TPU v7x, 32 devices: a whole 2x2x4 slice. The times are simulated.
32 devices in a mesh: slab: 2 (over y), col: 4 (over z), row: 2 (over x), ch: 2 (over core).
Axes of the slice: x: 2, y: 2, z: 4, core: 2. Of those that a mesh axis runs over, the one named last changes fastest.
Arguments:
- left_feat: bfloat16 [128, 128, 1024], P(('slab', 'row'), 'ch', 'col'), parts along dimension 0, may hold values from -512 to 512
- right_feat: bfloat16 [128, 128, 1024], P(('slab', 'row'), 'ch', 'col'), parts along dimension 0, may hold values from -12 to 12
- offsets: int32 [8], P(('slab', 'col')), parts along dimension 0, may hold values from 0 to 256, as said below
- valid: int32 [128, 1024], P(('slab', 'row'), ('col', 'ch')), parts along dimension 0, may hold values 0 or 1
- w_first: float32 [3, 3, 32, 2], replicated, may hold values from -1.5 to 1.5
- w_middle: float32 [3, 3, 32, 32], replicated, may hold values from -0.375 to 0.375
- w_last: float32 [3, 3, 1, 32], replicated, may hold values from -0.375 to 0.375
- grad_out: float32 [128, 1024], P(('slab', 'row'), ('col', 'ch')), parts along dimension 0, may hold values from -6 to 6
Outputs:
- refined: float32 [128, 1024], P(('slab', 'row'), ('col', 'ch')), parts along dimension 0
- grad_left: bfloat16 [128, 128, 1024], P(('slab', 'row'), 'ch', 'col'), parts along dimension 0
- grad_right: bfloat16 [128, 128, 1024], P(('slab', 'row'), 'ch', 'col'), parts along dimension 0
There are 2 independent parts, one for each index of `slab`. A program takes and returns all parts, laid end to end along the dimension named above; an argument that names none is the same for every part. Nothing has to cross between parts.
Inputs may be any that keep to these rules, and one draw needn't show every extreme that they name: `offsets`: the largest tile offset is exactly 256 in every draw.
All inputs are finite; a program needn't handle non-finite values. No bound on the sum of `valid` on one device may be relied on, other than what follows from the above.
Results may differ from a plain program's by a relative error of at most 0.005.
Values may be sent and summed in bfloat16 or wider, within the bound.
No kernel may reach another device: no remote copies, remote signals or barrier semaphores. Data moves between devices by JAX's collectives and lax.ppermute only.
A program may use at most 128 MiB of HBM per device.

v0:
```python
import functools
import math

import jax
import jax.numpy as jnp
import numpy as np
from jax import lax
from jax.experimental import pallas as pl
from jax.experimental.pallas import tpu as pltpu
from jax.sharding import PartitionSpec as P

DISP = 256
HALO = 4
LANES = 128
SIDE = 128
ALIGN = 16
NEG = -1e30
BAND = 400
GROUP = 4
F32 = jnp.float32
BF16 = jnp.bfloat16


def dot(a, b, dims=((1,), (0,))):
    return lax.dot_general(a, b, (dims, ((), ())), preferred_element_type=F32)


def band_tables(off):
    rem = (DISP + 1 - off) % ALIGN
    across = lax.broadcasted_iota(jnp.int32, (BAND, LANES), 1)
    down = lax.broadcasted_iota(jnp.int32, (BAND, LANES), 0)
    delta = across - down + (DISP - 1) + rem
    inside = (delta >= 0) & (delta < DISP)
    return delta.astype(F32) / DISP, jnp.where(inside, 0.0, NEG).astype(F32)


def band_start(off, block):
    rem = (DISP + 1 - off) % ALIGN
    return pl.multiple_of(LANES * block + DISP + 1 - off - rem, ALIGN)


def stats_body(chans, off_ref, lk, lo, r0k, r0o, r1k, r1o, r2k, r2o, grad_ref, keep_ref,
               field, top, bottom, stats, cost, level, mask, lines):
    step = pl.program_id(0)
    rate = math.log2(math.e) / math.sqrt(chans)
    off = off_ref[0]
    width = lk.shape[2]

    @pl.when(step == 0)
    def _():
        lev, msk = band_tables(off)
        level[...] = lev
        mask[...] = msk
        cost[3 * width:, :] = jnp.zeros((cost.shape[0] - 3 * width, width), F32)

    @pl.loop(0, GROUP)
    def _(row):
        left = jnp.concatenate([lk[row], lo[row]], axis=0)
        for slot, (own, other) in enumerate(((r2k, r2o), (r1k, r1o), (r0k, r0o))):
            right = jnp.concatenate([own[row], other[row]], axis=0)
            cost[slot * width:(slot + 1) * width, :] = dot(right, left, ((0,), (0,)))
        line = step * GROUP + row
        for block in range(width // LANES):
            cols = slice(block * LANES, (block + 1) * LANES)
            scores = cost[pl.ds(band_start(off, block), BAND), cols] + mask[...]
            top_score = jnp.max(scores, axis=0, keepdims=True)
            weight = jnp.exp2((scores - top_score) * rate)
            lev = level[...]
            total = jnp.sum(weight, axis=0, keepdims=True)
            mean = jnp.sum(weight * lev, axis=0, keepdims=True) / total
            apart = lev - mean
            spread = jnp.sum(weight * apart * apart, axis=0, keepdims=True) / total
            for at, value in enumerate((spread, top_score, mean, 1.0 / total)):
                lines[line, at:at + 1, cols] = value

    rows = field.shape[1]

    @pl.when(step == pl.num_programs(0) - 1)
    def _():
        for line in range(rows):
            for at in range(4):
                stats[at + 1, line:line + 1, :] = lines[line, at:at + 1, :]
        keep = keep_ref[...]
        coarse = stats[3] + off.astype(F32) / DISP
        stats[0] = coarse
        field[0] = coarse * keep
        field[1] = stats[1] * keep
        field[2] = grad_ref[...] * keep
        top[...] = field[:, :HALO, :]
        bottom[...] = field[:, rows - HALO:, :]


def group_spec(array):
    return pl.BlockSpec((GROUP,) + array.shape[1:], lambda i: (i, 0, 0))


def full_spec(shape):
    return pl.BlockSpec(shape, lambda i: (0,) * len(shape))


SMEM = pl.BlockSpec(memory_space=pltpu.SMEM)


def cost_of(flops, moved):
    return pl.CostEstimate(flops=flops, bytes_accessed=moved, transcendentals=0)


def band_stats(off, left, rights, grad_out, keep):
    rows, half, width = left[0].shape
    chans = 2 * half
    feats = list(left) + [part for pair in rights for part in pair]
    small = (rows, width)
    outs = ((3,) + small, (3, HALO, width), (3, HALO, width), (5,) + small)
    return pl.pallas_call(
        functools.partial(stats_body, chans),
        name="band_stats",
        grid=(rows // GROUP,),
        in_specs=[SMEM] + [group_spec(a) for a in feats] + [full_spec(small)] * 2,
        out_specs=[full_spec(s) for s in outs],
        out_shape=[jax.ShapeDtypeStruct(s, F32) for s in outs],
        scratch_shapes=[
            pltpu.VMEM((3 * width + ALIGN, width), F32),
            pltpu.VMEM((BAND, LANES), F32),
            pltpu.VMEM((BAND, LANES), F32),
            pltpu.VMEM((rows, 8, width), F32),
        ],
        cost_estimate=cost_of(2 * rows * 3 * width * width * chans, rows * 4 * width * chans * 2),
    )(off, *feats, grad_out, keep)


def left_body(chans, off_ref, lk, lo, r0k, r0o, r1k, r1o, r2k, r2o, coef, out_own, out_other,
              cost, slopes, level, mask):
    step = pl.program_id(0)
    rate = math.log2(math.e) / math.sqrt(chans)
    off = off_ref[0]
    width = lk.shape[2]

    @pl.when(step == 0)
    def _():
        lev, msk = band_tables(off)
        level[...] = lev
        mask[...] = msk
        cost[3 * width:, :] = jnp.zeros((cost.shape[0] - 3 * width, width), F32)
        slopes[...] = jnp.zeros(slopes.shape, BF16)

    @pl.loop(0, GROUP)
    def _(row):
        left = jnp.concatenate([lk[row], lo[row]], axis=0)
        rights = [jnp.concatenate([own[row], other[row]], axis=0)
                  for own, other in ((r2k, r2o), (r1k, r1o), (r0k, r0o))]
        for slot, right in enumerate(rights):
            cost[slot * width:(slot + 1) * width, :] = dot(right, left, ((0,), (0,)))
        at = step * GROUP + row
        for block in range(width // LANES):
            cols = slice(block * LANES, (block + 1) * LANES)
            where = pl.ds(band_start(off, block), BAND)
            top_score, mean, one, two, three = (coef[at, f:f + 1, cols] for f in range(5))
            weight = jnp.exp2((cost[where, cols] + mask[...] - top_score) * rate)
            apart = level[...] - mean
            slopes[where, cols] = (weight * (apart * (one + two * apart) - three)).astype(BF16)
        total = sum(dot(right, slopes[slot * width:(slot + 1) * width, :])
                    for slot, right in enumerate(rights))
        out_own[row] = total[:chans // 2].astype(BF16)
        out_other[row] = total[chans // 2:].astype(BF16)


def left_grads(off, left, rights, coef):
    rows, half, width = left[0].shape
    chans = 2 * half
    feats = list(left) + [part for pair in rights for part in pair]
    return pl.pallas_call(
        functools.partial(left_body, chans),
        name="left_grads",
        grid=(rows // GROUP,),
        in_specs=[SMEM] + [group_spec(a) for a in feats] + [full_spec(coef.shape)],
        out_specs=[group_spec(left[0])] * 2,
        out_shape=[jax.ShapeDtypeStruct(left[0].shape, BF16)] * 2,
        scratch_shapes=[
            pltpu.VMEM((3 * width + ALIGN, width), F32),
            pltpu.VMEM((3 * width + ALIGN, width), BF16),
            pltpu.VMEM((BAND, LANES), F32),
            pltpu.VMEM((BAND, LANES), F32),
        ],
        cost_estimate=cost_of(4 * rows * 3 * width * width * chans, rows * 5 * width * chans * 2),
    )(off, *feats, coef)


def right_body(chans, offs_ref, rk, ro, l0k, l0o, l1, l2, coef0, coef1, coef2,
               out_own, out_other, cost, slopes, mask):
    step = pl.program_id(0)
    rate = math.log2(math.e) / math.sqrt(chans)
    width = rk.shape[2]
    parts = width // LANES
    across = lax.broadcasted_iota(jnp.int32, (LANES, LANES), 1)
    down = lax.broadcasted_iota(jnp.int32, (LANES, LANES), 0)
    blocks = [(tile, col, row) for tile in range(3) for col in range(parts) for row in range(parts)]

    def base_of(tile, col, row):
        return tile * width + (col - row) * LANES - offs_ref[tile]

    def spot(tile, col, row):
        return (slice(row * LANES, (row + 1) * LANES),
                slice(tile * width + col * LANES, tile * width + (col + 1) * LANES))

    @pl.when(step == 0)
    def _():
        slopes[...] = jnp.zeros(slopes.shape, BF16)
        for tile, col, row in blocks:
            delta = across - down + base_of(tile, col, row)
            inside = (delta >= 0) & (delta < DISP)
            mask[spot(tile, col, row)] = jnp.where(inside, 0.0, NEG).astype(F32)

    @pl.loop(0, GROUP)
    def _(line):
        right = jnp.concatenate([rk[line], ro[line]], axis=0)
        lefts = [jnp.concatenate([l0k[line], l0o[line]], axis=0), l1[line], l2[line]]
        for tile, left in enumerate(lefts):
            cost[:, tile * width:(tile + 1) * width] = dot(right, left, ((0,), (0,)))
        at = step * GROUP + line
        table = (across - down).astype(F32) / DISP
        for tile, col, row in blocks:
            base = base_of(tile, col, row)

            @pl.when((base + LANES > 0) & (base - LANES < DISP))
            def _(tile=tile, col=col, row=row, base=base):
                here = spot(tile, col, row)
                cols = slice(col * LANES, (col + 1) * LANES)
                coef = (coef0, coef1, coef2)[tile]
                top_score, mean, one, two, three = (coef[at, f:f + 1, cols] for f in range(5))
                weight = jnp.exp2((cost[here] + mask[here] - top_score) * rate)
                apart = (table + base.astype(F32) / DISP) - mean
                slopes[here] = (weight * (apart * (one + two * apart) - three)).astype(BF16)

        total = sum(dot(left, slopes[:, tile * width:(tile + 1) * width], ((1,), (1,)))
                    for tile, left in enumerate(lefts))
        out_own[line] = total[:chans // 2].astype(BF16)
        out_other[line] = total[chans // 2:].astype(BF16)


def right_grads(offs, right, left, left_one, left_two, coefs):
    rows, half, width = right[0].shape
    chans = 2 * half
    feats = list(right) + list(left) + [left_one, left_two]
    return pl.pallas_call(
        functools.partial(right_body, chans),
        name="right_grads",
        grid=(rows // GROUP,),
        in_specs=[SMEM] + [group_spec(a) for a in feats] + [full_spec(a.shape) for a in coefs],
        out_specs=[group_spec(right[0])] * 2,
        out_shape=[jax.ShapeDtypeStruct(right[0].shape, BF16)] * 2,
        scratch_shapes=[
            pltpu.VMEM((width, 3 * width), F32),
            pltpu.VMEM((width, 3 * width), BF16),
            pltpu.VMEM((width, 3 * width), F32),
        ],
        cost_estimate=cost_of(4 * rows * 3 * width * width * chans, rows * 5 * width * chans * 2),
    )(offs, *feats, *coefs)


def split_halves(values):
    high = values.astype(BF16)
    return high, (values - high.astype(F32)).astype(BF16)


def fine_dot(weights, high, low):
    w_high, w_low = weights
    return dot(w_high, high) + dot(w_high, low) + dot(w_low, high)


def tap_rows(values):
    last = values.shape[1] - 1
    return jnp.concatenate([pltpu.roll(values, 1, 1), values, pltpu.roll(values, last, 1)], axis=0)


def merge_taps(stacked):
    count, lanes = stacked.shape[0] // 3, stacked.shape[1]
    return (pltpu.roll(stacked[:count], 1, 1) + stacked[count:2 * count]
            + pltpu.roll(stacked[2 * count:], lanes - 1, 1))


def refine_body(chans, hid, flags, field, above, below, side, stats, keep_ref,
                w_one, w_two, w_three, w_three_back, w_two_back, w_one_back,
                refined, coef, wide, one_high, one_low, slope_one,
                two_high, two_low, slope_two, g_two_high, g_two_low, g_one_high, g_one_low):
    rows, width = field.shape[1:]
    ext = rows + 2 * HALO
    lanes = width + SIDE
    for f in range(3):
        base = f * ext
        wide[base:base + HALO, :width] = above[f]
        wide[base + HALO:base + HALO + rows, :width] = field[f]
        wide[base + HALO + rows:base + ext, :width] = below[f]
        wide[base:base + ext, width:] = side[f]

    def present(first, count):
        line = first + lax.broadcasted_iota(jnp.int32, (count * hid, lanes), 0) // hid
        lane = lax.broadcasted_iota(jnp.int32, (count * hid, lanes), 1)
        low = HALO * flags[0]
        high = ext - HALO * flags[1]
        start = lanes - (SIDE // 2) * (1 - flags[2])
        end = width + (SIDE // 2) * (1 - flags[3])
        return (line >= low) & (line < high) & ((lane < end) | (lane >= start))

    def gate(values):
        return 1.0 / (1.0 + jnp.exp(-values))

    def activate(values, first, count, high_ref, low_ref, slope_ref, at):
        sig = gate(values)
        ok = present(first, count)
        hidden = jnp.where(ok, values * sig, 0.0)
        slope_ref[at] = jnp.where(ok, sig * (1.0 + values * (1.0 - sig)), 0.0)
        high_ref[at], low_ref[at] = split_halves(hidden)

    piece = 6
    taps = split_halves(tap_rows(wide[:2 * ext, :]))
    for part in range(ext // piece):
        at = slice(part * piece * hid, (part + 1) * piece * hid)
        values = fine_dot(split_halves(w_one[at, :]), *taps)
        activate(values, part * piece, piece, one_high, one_low, slope_one, at)

    count = ext - 4
    wt = split_halves(w_two[...])
    piece = w_two.shape[0] // (3 * hid)
    for part in range(count // piece):
        source = slice((part * piece + 1) * hid, (part * piece + 1) * hid + w_two.shape[1])
        values = merge_taps(fine_dot(wt, one_high[source], one_low[source]))
        at = slice(part * piece * hid, (part + 1) * piece * hid)
        activate(values, part * piece + 2, piece, two_high, two_low, slope_two, at)

    inner = slice(hid, (count - 1) * hid)
    out = merge_taps(fine_dot(split_halves(w_three[...]), two_high[inner], two_low[inner]))
    keep = keep_ref[...]
    refined[...] = keep * (stats[0] + out[:, :width])

    taps = split_halves(tap_rows(wide[2 * ext:, :]))
    for part in range(count // piece):
        at = slice(part * piece * hid, (part + 1) * piece * hid)
        grads = fine_dot(split_halves(w_three_back[at, :]), *taps) * slope_two[at]
        g_two_high[at], g_two_low[at] = split_halves(grads)

    wt = split_halves(w_two_back[...])
    piece = w_two_back.shape[0] // (3 * hid)
    for part in range((count - 2) // piece):
        source = slice(part * piece * hid, part * piece * hid + w_two_back.shape[1])
        at = slice(part * piece * hid, (part + 1) * piece * hid)
        over = slice((part * piece + 3) * hid, (part * piece + 3 + piece) * hid)
        grads = merge_taps(fine_dot(wt, g_two_high[source], g_two_low[source])) * slope_one[over]
        g_one_high[at], g_one_low[at] = split_halves(grads)

    back = merge_taps(fine_dot(split_halves(w_one_back[...]), g_one_high[...], g_one_low[...]))
    for_coarse = field[2] + back[:rows, :width] * keep
    for_spread = back[rows:, :width] * keep
    scale = stats[4] / math.sqrt(chans)
    planes = (stats[2], stats[3], for_coarse * scale, for_spread * scale,
              for_spread * stats[1] * scale, jnp.full((rows, width), flags[4], jnp.int32).astype(F32))
    coef[...] = jnp.zeros(coef.shape, F32)
    for at, plane in enumerate(planes):
        for line in range(rows):
            coef[line, at:at + 1, :] = plane[line:line + 1, :]


def near(out_rows, in_rows, shift):
    gap = np.arange(in_rows)[None, :] - np.arange(out_rows)[:, None] + shift
    return [(gap == tap).astype(np.float32) for tap in range(3)]


def expand(weights, out_rows, in_rows, shift, order):
    table = near(out_rows, in_rows, shift)
    full = sum(jnp.asarray(table[tap])[None, :, None, :, None] * weights[tap][:, None, :, None, :]
               for tap in range(3))
    return jnp.transpose(full, order)


def refine_weights(w_first, w_middle, w_last, rows):
    ext = rows + 2 * HALO
    hid, ins = w_first.shape[2:]

    def turned(w):
        return jnp.transpose(w[::-1, ::-1], (0, 1, 3, 2))

    one = expand(w_first, ext, ext, 1, (1, 2, 0, 4, 3)).reshape(ext * hid, 3 * ins * ext)
    two = expand(w_middle, 5, 7, 0, (0, 1, 2, 3, 4)).reshape(3 * 5 * hid, 7 * hid)
    three = expand(w_last, rows, rows + 2, 0, (0, 1, 2, 3, 4)).reshape(3 * rows, (rows + 2) * hid)
    three_back = expand(turned(w_last), ext - 4, ext, -1, (1, 2, 0, 4, 3)).reshape(
        (ext - 4) * hid, 3 * ext)
    two_back = expand(turned(w_middle), 6, 8, 0, (0, 1, 2, 3, 4)).reshape(3 * 6 * hid, 8 * hid)
    one_back = expand(turned(w_first), rows, rows + 2, 0, (0, 2, 1, 3, 4)).reshape(
        3 * ins * rows, (rows + 2) * hid)
    return one, two, three, three_back, two_back, one_back


def refine(flags, field, above, below, side, stats, keep, weights, chans, hid):
    rows, width = field.shape[1:]
    ext, lanes = rows + 2 * HALO, width + SIDE
    small = (rows, width)
    vmem = pl.BlockSpec(memory_space=pltpu.VMEM)
    outs = (small, (rows, 8, width))

    def both(count):
        return [pltpu.VMEM((count * hid, lanes), BF16)] * 2

    def single(count):
        return [pltpu.VMEM((count * hid, lanes), F32)]

    return pl.pallas_call(
        functools.partial(refine_body, chans, hid),
        name="refine",
        in_specs=[SMEM] + [vmem] * 12,
        out_specs=[vmem] * 2,
        out_shape=[jax.ShapeDtypeStruct(s, F32) for s in outs],
        scratch_shapes=[pltpu.VMEM((3 * ext, lanes), F32)] + both(ext) + single(ext)
        + both(ext - 4) + single(ext - 4) + both(ext - 4) + both(ext - 6),
        cost_estimate=cost_of(4 * 10 ** 9, 8 * 10 ** 6),
    )(flags, field, above, below, side, stats, keep, *weights)


def shards(left_feat, right_feat, offsets, valid, w_first, w_middle, w_last, grad_out):
    cols, rows2 = lax.axis_size("col"), lax.axis_size("row") * lax.axis_size("ch")
    col, core = lax.axis_index("col"), lax.axis_index("ch")
    band = lax.axis_index("row") * lax.axis_size("ch") + core
    chans = left_feat.shape[1] * lax.axis_size("ch")
    hid = w_first.shape[2]
    rows = left_feat.shape[0] // 2
    width = left_feat.shape[2]

    def keep_part(a, axis=0):
        count = a.shape[axis] // 2
        return lax.dynamic_slice_in_dim(a, core * count, count, axis)

    def give_part(a, axis=0):
        count = a.shape[axis] // 2
        return lax.dynamic_slice_in_dim(a, (1 - core) * count, count, axis)

    def swap(a):
        return lax.ppermute(a, "ch", [(0, 1), (1, 0)])

    def joined(own, other, axis):
        return jnp.where(core == 0, jnp.concatenate([own, other], axis),
                         jnp.concatenate([other, own], axis))

    def over_cols(a, step):
        pairs = [(i, i + step) for i in range(cols) if 0 <= i + step < cols]
        return lax.ppermute(a, "col", pairs)

    def crossed(a, step):
        pairs = [(2 * i + j, 2 * (i + step) + 1 - j)
                 for i in range(cols) if 0 <= i + step < cols for j in range(2)]
        return lax.ppermute(a, ("col", "ch"), pairs)

    def over_rows(a, step):
        pairs = [(i, i + step) for i in range(rows2) if 0 <= i + step < rows2]
        return lax.ppermute(a, ("row", "ch"), pairs)

    left_own, left_give = keep_part(left_feat), give_part(left_feat)
    right_own, right_give = keep_part(right_feat), give_part(right_feat)
    one_own = over_cols(right_own, 1)
    one_other = crossed(right_give, 1)
    left_other, right_other = swap(left_give), swap(right_give)
    left_all = jnp.concatenate([left_own, left_other], axis=1)
    left_one = over_cols(left_all, -1)
    two_own = over_cols(one_own, 1)
    two_other = over_cols(one_other, 1)
    left_two = over_cols(left_one, -1)

    maps = jnp.stack([grad_out, valid.astype(F32)])
    maps = joined(keep_part(maps, 1), swap(give_part(maps, 1)), 2)
    grad_map, keep = maps[0], maps[1]
    weights = refine_weights(w_first, w_middle, w_last, rows)

    rights = ((right_own, right_other), (one_own, one_other), (two_own, two_other))
    left = (left_own, left_other)
    field, top, bottom, stats = band_stats(offsets, left, rights, grad_map, keep)

    above, below = over_rows(bottom, 1), over_rows(top, -1)
    first = jnp.concatenate([above[:, :, :HALO], field[:, :, :HALO], below[:, :, :HALO]], axis=1)
    final = jnp.concatenate([a[:, :, width - HALO:] for a in (above, field, below)], axis=1)
    before, after = over_cols(final, 1), over_cols(first, -1)
    gap = jnp.zeros(after.shape[:2] + (SIDE - 2 * HALO,), F32)
    side = jnp.concatenate([after, gap, before], axis=2)
    flags = jnp.stack([band == 0, band == rows2 - 1, col == 0, col == cols - 1]).astype(jnp.int32)
    flags = jnp.concatenate([flags, offsets])
    refined, coef = refine(flags, field, above, below, side, stats, keep, weights, chans, hid)

    coef_one, coef_two = over_cols(coef, -1), over_cols(coef, -2)
    grad_left = left_grads(offsets, left, rights, coef)
    grad_left = joined(grad_left[0], swap(grad_left[1]), 0)
    offs = jnp.stack([offsets[0], coef_one[0, 5, 0].astype(jnp.int32),
                      coef_two[0, 5, 0].astype(jnp.int32)])
    grad_right = right_grads(offs, rights[0], left, left_one, left_two, (coef, coef_one, coef_two))
    grad_right = joined(grad_right[0], swap(grad_right[1]), 0)
    refined = joined(keep_part(refined, 1), swap(give_part(refined, 1)), 0)
    return (refined, grad_left, grad_right)


def solution(mesh):
    placed = (
        P(("slab", "row"), "ch", "col"),
        P(("slab", "row"), "ch", "col"),
        P(("slab", "col")),
        P(("slab", "row"), ("col", "ch")),
        P(),
        P(),
        P(),
        P(("slab", "row"), ("col", "ch")),
    )
    return jax.shard_map(
        shards,
        mesh=mesh,
        in_specs=placed,
        out_specs=(placed[3], placed[0], placed[0]),
        check_vma=False,
    )
```

profile of v0, /device:TPU:17, one launch (start us, length us, event | category | flops | bytes accessed | tf_op | source)
XLA Modules:
  0.0 156.6 jit_solution(8095834172419240666)
XLA Ops:
  0.7 2.4 %constant_dynamic-slice_fusion.2 = (bf16[16,64,256]{2,1,0:T(8,128)(2,1)}, bf16[16,64,256]{2,1,0:T(8,128)(2,1)}) fusion(bf16[32,64,256]{2,1,0:T(8,128)(2,1)} %param.27, s32[]{:T(128)S(6)} %select_n.46, s32[]{:T(128)S(6)} %select_n.45), kind=kLoop, calls=%fused_computation.39 | loop fusion | bytes 2097160 | tf_op jit(solution)/shard_map/dynamic_slice | solution.py:432
  3.1 3.8 %collective-permute-start.3 = (bf16[16,64,256]{2,1,0:T(8,128)(2,1)}, bf16[16,64,256]{2,1,0:T(8,128)(2,1)}, u32[]{:S(2)}, u32[]{:S(2)}) collective-permute-start(bf16[16,64,256]{2,1,0:T(8,128)(2,1)} %get-tuple-element.23), channel_id=1, source_target_pairs={{0,5},{1,4},{4,9},{5,8},{8,13},{9,12},{2,7},{3,6},{6,11},{7,10},{1... | collective-permute-start | bytes 1572872 | tf_op jit(solution)/shard_map/ppermute | solution.py:448
  8.1 2.0 %collective-permute-start.2 = (bf16[16,64,256]{2,1,0:T(8,128)(2,1)}, bf16[16,64,256]{2,1,0:T(8,128)(2,1)}, u32[]{:S(2)}, u32[]{:S(2)}) collective-permute-start(bf16[16,64,256]{2,1,0:T(8,128)(2,1)} %get-tuple-element.24.r0k.rk), channel_id=1, source_target_pairs={{0,4},{4,8},{8,12},{1,5},{5,9},{9,13},{2,6},{6,10},{10,14},{3,7},{... | collective-permute-start | bytes 1572872 | tf_op jit(solution)/shard_map/ppermute | solution.py:443
  14.1 1.6 %multiply_add_fusion.2 = f32[24,32,3,2,24]{1,0,4,3,2:T(8,128)} fusion(f32[32,3,2]{0,2,1:T(2,128)S(1)} %get-tuple-element.50, f32[24,24]{0,1:T(8,128)S(1)} %copy-done.14, f32[32,3,2]{0,2,1:T(2,128)S(1)} %get-tuple-element.49, f32[24,24]{0,1:T(8,128)S(1)} %copy-done.13, f32[32,3,2]{0,2,1:T(2,128)S(1)} %get-tuple-element.48, f32[24,24]{0,1:T(8,128)S(1)} %copy-done.12), kind=kLoop, calls=%fused_computation.2 | loop fusion | flops 552960 | bytes 451584 | tf_op jit(solution)/shard_map/add | solution.py:369
  15.7 1.7 %multiply_add_fusion.1 = f32[3,5,32,7,32]{4,3,2,1,0:T(8,128)} fusion(f32[3,32,32]{2,1,0:T(8,128)S(1)} %get-tuple-element.32, f32[5,7]{1,0:T(8,128)S(1)} %copy-done.23, f32[3,32,32]{2,1,0:T(8,128)S(1)} %get-tuple-element.31, f32[5,7]{1,0:T(8,128)S(1)} %copy-done.22, f32[3,32,32]{2,1,0:T(8,128)S(1)} %get-tuple-element.30, f32[5,7]{1,0:T(8,128)S(1)} %copy-done.21), kind=kLoop, calls=%fused_computation.1 | loop fusion | flops 537600 | bytes 467364 | tf_op jit(solution)/shard_map/add | solution.py:369
  19.5 1.3 multiply_add_fusion
  20.9 10.1 %collective-permute-done.2.r1k = bf16[16,64,256]{2,1,0:T(8,128)(2,1)} collective-permute-done((bf16[16,64,256]{2,1,0:T(8,128)(2,1)}, bf16[16,64,256]{2,1,0:T(8,128)(2,1)}, u32[]{:S(2)}, u32[]{:S(2)}) %collective-permute-start.2) | collective-permute-done | bytes 524320 | tf_op jit(solution)/shard_map/ppermute | solution.py:443
  31.0 3.2 %collective-permute-start.4 = (bf16[16,64,256]{2,1,0:T(8,128)(2,1)}, bf16[16,64,256]{2,1,0:T(8,128)(2,1)}, u32[]{:S(2)}, u32[]{:S(2)}) collective-permute-start(bf16[16,64,256]{2,1,0:T(8,128)(2,1)} %collective-permute-done.2.r1k), channel_id=1, source_target_pairs={{0,4},{4,8},{8,12},{1,5},{5,9},{9,13},{2,6},{6,10},{10,14},{3,7},{... | collective-permute-start | bytes 1572872 | tf_op jit(solution)/shard_map/ppermute | solution.py:443
  34.2 1.9 %collective-permute-start.5 = (bf16[16,64,256]{2,1,0:T(8,128)(2,1)}, bf16[16,64,256]{2,1,0:T(8,128)(2,1)}, u32[]{:S(2)}, u32[]{:S(2)}) collective-permute-start(bf16[16,64,256]{2,1,0:T(8,128)(2,1)} %collective-permute-done.3.r1o), channel_id=1, source_target_pairs={{0,4},{4,8},{8,12},{1,5},{5,9},{9,13},{2,6},{6,10},{10,14},{3,7},{... | collective-permute-start | bytes 1572872 | tf_op jit(solution)/shard_map/ppermute | solution.py:443
  38.2 2.3 %pad_maximum_fusion = bf16[16,128,256]{2,1,0:T(8,128)(2,1)} fusion(bf16[16,64,256]{2,1,0:T(8,128)(2,1)} %collective-permute-done.lo.l0o, bf16[16,64,256]{2,1,0:T(8,128)(2,1)} %get-tuple-element.26.lk.l0k), kind=kLoop, calls=%fused_computation.5 | loop fusion | flops 2097152 | bytes 2097152 | tf_op jit(solution)/shard_map/concatenate | solution.py:459
  40.5 3.4 %collective-permute-start.15 = (bf16[16,128,256]{2,1,0:T(8,128)(2,1)}, bf16[16,128,256]{2,1,0:T(8,128)(2,1)}, u32[]{:S(2)}, u32[]{:S(2)}) collective-permute-start(bf16[16,128,256]{2,1,0:T(8,128)(2,1)} %pad_maximum_fusion), channel_id=1, source_target_pairs={{4,0},{8,4},{12,8},{5,1},{9,5},{13,9},{6,2},{10,6},{14,10},{7,3},{... | collective-permute-start | bytes 3145736 | tf_op jit(solution)/shard_map/ppermute | solution.py:443
  44.4 1.8 %collective-permute-done.4.r2k = bf16[16,64,256]{2,1,0:T(8,128)(2,1)} collective-permute-done((bf16[16,64,256]{2,1,0:T(8,128)(2,1)}, bf16[16,64,256]{2,1,0:T(8,128)(2,1)}, u32[]{:S(2)}, u32[]{:S(2)}) %collective-permute-start.4) | collective-permute-done | bytes 524320 | tf_op jit(solution)/shard_map/ppermute | solution.py:443
  46.3 11.2 %collective-permute-done.5.r2o = bf16[16,64,256]{2,1,0:T(8,128)(2,1)} collective-permute-done((bf16[16,64,256]{2,1,0:T(8,128)(2,1)}, bf16[16,64,256]{2,1,0:T(8,128)(2,1)}, u32[]{:S(2)}, u32[]{:S(2)}) %collective-permute-start.5) | collective-permute-done | bytes 524320 | tf_op jit(solution)/shard_map/ppermute | solution.py:443
  57.5 10.6 %band_stats.1 = (f32[3,16,256]{2,1,0:T(8,128)}, f32[3,4,256]{2,1,0:T(4,128)}, f32[3,4,256]{2,1,0:T(4,128)}, f32[5,16,256]{2,1,0:T(8,128)}) custom-call(s32[1]{0:T(128)S(6)} %copy.75.off_ref, bf16[16,64,256]{2,1,0:T(8,128)(2,1)} %get-tuple-element.26.lk.l0k, bf16[16,64,256]{2,1,0:T(8,128)(2,1)} %collective-permute-done.lo.l0o, ...), custom_call_target="tpu_custom_call" | custom-call | flops 805306368 | bytes 4194304 | tf_op jit(solution)/shard_map/band_stats/pallas_call | solution.py:114
  68.1 4.3 %collective-permute-start.7 = (f32[3,4,256]{2,1,0:T(4,128)}, f32[3,4,256]{2,1,0:T(4,128)S(1)}, u32[]{:S(2)}, u32[]{:S(2)}) collective-permute-start(f32[3,4,256]{2,1,0:T(4,128)} %get-tuple-element.14), channel_id=1, source_target_pairs={{0,1},{1,2},{2,3},{4,5},{5,6},{6,7},{8,9},{9,10},{10,11},{12,13},{... | collective-permute-start | bytes 36872 | tf_op jit(solution)/shard_map/ppermute | solution.py:452
  73.2 1.9 %collective-permute-start.8 = (f32[3,4,256]{2,1,0:T(4,128)}, f32[3,4,256]{2,1,0:T(4,128)S(1)}, u32[]{:S(2)}, u32[]{:S(2)}) collective-permute-start(f32[3,4,256]{2,1,0:T(4,128)} %get-tuple-element.15), channel_id=1, source_target_pairs={{1,0},{2,1},{3,2},{5,4},{6,5},{7,6},{9,8},{10,9},{11,10},{13,12},{... | collective-permute-start | bytes 36872 | tf_op jit(solution)/shard_map/ppermute | solution.py:452
  75.2 3.2 %collective-permute-done.8.below = f32[3,4,256]{2,1,0:T(4,128)S(1)} collective-permute-done((f32[3,4,256]{2,1,0:T(4,128)}, f32[3,4,256]{2,1,0:T(4,128)S(1)}, u32[]{:S(2)}, u32[]{:S(2)}) %collective-permute-start.8) | collective-permute-done | bytes 12320 | tf_op jit(solution)/shard_map/ppermute | solution.py:452
  79.1 2.1 %collective-permute-start.9 = (f32[3,24,4]{2,1,0:T(8,128)}, f32[3,24,4]{2,1,0:T(8,128)}, u32[]{:S(2)}, u32[]{:S(2)}) collective-permute-start(f32[3,24,4]{2,1,0:T(8,128)} %pad_maximum_fusion.1), channel_id=1, source_target_pairs={{4,0},{8,4},{12,8},{5,1},{9,5},{13,9},{6,2},{10,6},{14,10},{7,3},{... | collective-permute-start | bytes 3464 | tf_op jit(solution)/shard_map/ppermute | solution.py:443
  81.2 1.9 %collective-permute-start.16 = (bf16[16,128,256]{2,1,0:T(8,128)(2,1)}, bf16[16,128,256]{2,1,0:T(8,128)(2,1)}, u32[]{:S(2)}, u32[]{:S(2)}) collective-permute-start(bf16[16,128,256]{2,1,0:T(8,128)(2,1)} %collective-permute-done.15.l1), channel_id=1, source_target_pairs={{4,0},{8,4},{12,8},{5,1},{9,5},{13,9},{6,2},{10,6},{14,10},{7,3},{... | collective-permute-start | bytes 3145736 | tf_op jit(solution)/shard_map/ppermute | solution.py:443
  83.8 4.5 %collective-permute-start.10 = (f32[3,24,4]{2,1,0:T(8,128)}, f32[3,24,4]{2,1,0:T(8,128)}, u32[]{:S(2)}, u32[]{:S(2)}) collective-permute-start(f32[3,24,4]{2,1,0:T(8,128)} %pad_maximum_fusion.2), channel_id=1, source_target_pairs={{0,4},{4,8},{8,12},{1,5},{5,9},{9,13},{2,6},{6,10},{10,14},{3,7},{... | collective-permute-start | bytes 3464 | tf_op jit(solution)/shard_map/ppermute | solution.py:443
  88.9 2.1 %reshape.164 = f32[640,72]{0,1:T(8,128)} reshape(f32[20,32,3,1,24]{1,0,4,2,3:T(8,128)} %add_bitcast_fusion) | data formatting | bytes 368640 | tf_op jit(solution)/shard_map/reshape | solution.py:384
  91.0 1.8 %copy.60.w_three_back = f32[640,72]{1,0:T(8,128)} copy(f32[640,72]{0,1:T(8,128)} %reshape.164) | data formatting | bytes 368640 | tf_op jit(solution)/shard_map/reshape | solution.py:384
  92.8 1.9 %add.120.w_three = f32[48,576]{1,0:T(8,128)} reshape(f32[3,16,18,32]{3,2,1,0:T(8,128)} %multiply_add_fusion.4) | data formatting | bytes 221184 | tf_op jit(solution)/shard_map/add | solution.py:369
  94.6 1.5 add.125.w_two_back
  96.1 2.9 %add.114 = f32[768,144]{0,1:T(8,128)} reshape(f32[24,32,3,2,24]{1,0,4,3,2:T(8,128)} %multiply_add_fusion.2) | data formatting | bytes 884736 | tf_op jit(solution)/shard_map/add | solution.py:369
  99.0 2.2 %copy.59.w_one = f32[768,144]{1,0:T(8,128)} copy(f32[768,144]{0,1:T(8,128)} %add.114) | data formatting | bytes 884736 | tf_op jit(solution)/shard_map/add | solution.py:369
  103.5 1.5 pad_maximum_fusion.3.side
  105.0 8.2 %refine.1 = (f32[16,256]{1,0:T(8,128)}, f32[16,8,256]{2,1,0:T(8,128)}) custom-call(s32[5]{0:T(128)} %pad_add_fusion.flags, f32[3,16,256]{2,1,0:T(8,128)} %get-tuple-element.13.field, f32[3,4,256]{2,1,0:T(4,128)} %copy-done.18, f32[3,4,256]{2,1,0:T(4,128)} %copy-done.19, f32[3,24,128]{2,1,0:T(8,128)} %pad_maximum_fusion.3.side, ...), custom_call_target="tpu_custom_call" | custom-call | flops 4000000000 | bytes 8000000 | tf_op jit(solution)/shard_map/refine/pallas_call | solution.py:405
  113.2 1.9 %collective-permute-start.13 = (f32[16,8,256]{2,1,0:T(8,128)}, f32[16,8,256]{2,1,0:T(8,128)S(1)}, u32[]{:S(2)}, u32[]{:S(2)}) collective-permute-start(f32[16,8,256]{2,1,0:T(8,128)} %get-tuple-element.18.coef.coef0), channel_id=1, source_target_pairs={{4,0},{8,4},{12,8},{5,1},{9,5},{13,9},{6,2},{10,6},{14,10},{7,3},{... | collective-permute-start | bytes 393224 | tf_op jit(solution)/shard_map/ppermute | solution.py:443
  116.4 14.4 %left_grads.1 = (bf16[16,64,256]{2,1,0:T(8,128)(2,1)}, bf16[16,64,256]{2,1,0:T(8,128)(2,1)}) custom-call(s32[1]{0:T(128)S(6)} %copy.75.off_ref, bf16[16,64,256]{2,1,0:T(8,128)(2,1)} %get-tuple-element.26.lk.l0k, bf16[16,64,256]{2,1,0:T(8,128)(2,1)} %collective-permute-done.lo.l0o, bf16[16,64,256]{2,1,0:T(8,128)(2,1)} %get-tuple-element.24.r0k.rk, ...), custom_call_target="tpu_custom_call" | custom-call | flops 1610612736 | bytes 5242880 | tf_op jit(solution)/shard_map/left_grads/pallas_call | solution.py:171
  133.9 17.4 %right_grads.1 = (bf16[16,64,256]{2,1,0:T(8,128)(2,1)}, bf16[16,64,256]{2,1,0:T(8,128)(2,1)}) custom-call(s32[3]{0:T(128)} %pad_add_fusion.1.offs_ref, bf16[16,64,256]{2,1,0:T(8,128)(2,1)} %get-tuple-element.24.r0k.rk, bf16[16,64,256]{2,1,0:T(8,128)(2,1)} %collective-permute-done.1.r0o.ro, bf16[16,64,256]{2,1,0:T(8,128)(2,1)} %get-tuple-element.26.lk.l0k, ...), custom_call_target="tpu_custom_call" | custom-call | flops 1610612736 | bytes 5242880 | tf_op jit(solution)/shard_map/right_grads/pallas_call | solution.py:244
  152.0 1.6 %collective-permute-done.11 = f32[16,128]{1,0:T(8,128)S(1)} collective-permute-done((f32[16,128]{1,0:T(8,128)S(1)}, f32[16,128]{1,0:T(8,128)S(1)}, u32[]{:S(2)}, u32[]{:S(2)}) %collective-permute-start.11) | collective-permute-done | bytes 8224 | tf_op jit(solution)/shard_map/ppermute | solution.py:435
  (117 shorter events, 20.9 us)
Async XLA Ops:
  0.6 6.3 %copy-start.9 = (s32[32,128]{1,0:T(8,128)S(1)}, s32[32,128]{1,0:T(8,128)}, u32[]{:S(2)}) copy-start(s32[32,128]{1,0:T(8,128)} %param.29) | copy-start | bytes 49156
  0.6 6.3 %copy-start.11 = (f32[32,128]{1,0:T(8,128)S(1)}, f32[32,128]{1,0:T(8,128)}, u32[]{:S(2)}) copy-start(f32[32,128]{1,0:T(8,128)} %param.33) | copy-start | bytes 49156
  0.7 9.5 %copy-start.1 = (bf16[32,64,256]{2,1,0:T(8,128)(2,1)S(1)}, bf16[32,64,256]{2,1,0:T(8,128)(2,1)}, u32[]{:S(2)}) copy-start(bf16[32,64,256]{2,1,0:T(8,128)(2,1)} %param.26) | copy-start | bytes 3145732
  0.7 10.6 %copy-start.20 = (f32[3,3,1,32]{3,2,1,0:T(1,128)S(1)}, f32[3,3,1,32]{3,2,1,0:T(1,128)}, u32[]{:S(2)}) copy-start(f32[3,3,1,32]{3,2,1,0:T(1,128)} %param.32) | copy-start | bytes 3460
  0.7 10.7 %copy-start.5 = (f32[3,3,32,2]{2,3,1,0:T(2,128)S(1)}, f32[3,3,32,2]{2,3,1,0:T(2,128)}, u32[]{:S(2)}) copy-start(f32[3,3,32,2]{2,3,1,0:T(2,128)} %param.30) | copy-start | bytes 6916
  0.7 10.7 %copy-start.2 = (f32[3,3,32,32]{3,2,1,0:T(8,128)S(1)}, f32[3,3,32,32]{3,2,1,0:T(8,128)}, u32[]{:S(2)}) copy-start(f32[3,3,32,32]{3,2,1,0:T(8,128)} %param.31) | copy-start | bytes 110596
  0.7 10.8 %copy-start.6 = (f32[16,18]{1,0:T(8,128)S(1)}, f32[16,18]{1,0:T(8,128)}, u32[]{:S(2)}) copy-start(f32[16,18]{1,0:T(8,128)} %constant.65.clone) | copy-start | bytes 3460
  0.7 10.8 %copy-start.7 = (f32[16,18]{1,0:T(8,128)S(1)}, f32[16,18]{1,0:T(8,128)}, u32[]{:S(2)}) copy-start(f32[16,18]{1,0:T(8,128)} %constant.66.clone) | copy-start | bytes 3460
  0.7 10.8 %copy-start.8 = (f32[16,18]{1,0:T(8,128)S(1)}, f32[16,18]{1,0:T(8,128)}, u32[]{:S(2)}) copy-start(f32[16,18]{1,0:T(8,128)} %constant.67.clone) | copy-start | bytes 3460
  3.1 31.1 %collective-permute-start.3 = (bf16[16,64,256]{2,1,0:T(8,128)(2,1)}, bf16[16,64,256]{2,1,0:T(8,128)(2,1)}, u32[]{:S(2)}, u32[]{:S(2)}) collective-permute-start(bf16[16,64,256]{2,1,0:T(8,128)(2,1)} %get-tuple-element.23), channel_id=1, source_target_pairs={{0,5},{1,4},{4,9},{5,8},{8,13},{9,12},{2,7},{3,6},{6,11},{7,10},{1... | collective-permute-start | bytes 1572872 | tf_op jit(solution)/shard_map/ppermute | solution.py:448
  6.9 37.6 %collective-permute-start.1 = (bf16[16,64,256]{2,1,0:T(8,128)(2,1)}, bf16[16,64,256]{2,1,0:T(8,128)(2,1)}, u32[]{:S(2)}, u32[]{:S(2)}) collective-permute-start(bf16[16,64,256]{2,1,0:T(8,128)(2,1)} %get-tuple-element.23), channel_id=1, source_target_pairs={{0,1},{1,0},{2,3},{3,2},{4,5},{5,4},{6,7},{7,6},{8,9},{9,8},{10,11... | collective-permute-start | bytes 1572872 | tf_op jit(solution)/shard_map/ppermute | solution.py:435
  7.6 29.8 %collective-permute-start.6 = (f32[2,16,128]{2,1,0:T(8,128)}, f32[2,16,128]{2,1,0:T(8,128)}, u32[]{:S(2)}, u32[]{:S(2)}) collective-permute-start(f32[2,16,128]{2,1,0:T(8,128)} %get-tuple-element.38), channel_id=1, source_target_pairs={{0,1},{1,0},{2,3},{3,2},{4,5},{5,4},{6,7},{7,6},{8,9},{9,8},{10,11... | collective-permute-start | bytes 49160 | tf_op jit(solution)/shard_map/ppermute | solution.py:435
  8.1 22.9 %collective-permute-start.2 = (bf16[16,64,256]{2,1,0:T(8,128)(2,1)}, bf16[16,64,256]{2,1,0:T(8,128)(2,1)}, u32[]{:S(2)}, u32[]{:S(2)}) collective-permute-start(bf16[16,64,256]{2,1,0:T(8,128)(2,1)} %get-tuple-element.24.r0k.rk), channel_id=1, source_target_pairs={{0,4},{4,8},{8,12},{1,5},{5,9},{9,13},{2,6},{6,10},{10,14},{3,7},{... | collective-permute-start | bytes 1572872 | tf_op jit(solution)/shard_map/ppermute | solution.py:443
  11.3 26.9 %collective-permute-start = (bf16[16,64,256]{2,1,0:T(8,128)(2,1)}, bf16[16,64,256]{2,1,0:T(8,128)(2,1)}, u32[]{:S(2)}, u32[]{:S(2)}) collective-permute-start(bf16[16,64,256]{2,1,0:T(8,128)(2,1)} %get-tuple-element.25), channel_id=1, source_target_pairs={{0,1},{1,0},{2,3},{3,2},{4,5},{5,4},{6,7},{7,6},{8,9},{9,8},{10,11... | collective-permute-start | bytes 1572872 | tf_op jit(solution)/shard_map/ppermute | solution.py:435
  31.0 15.3 %collective-permute-start.4 = (bf16[16,64,256]{2,1,0:T(8,128)(2,1)}, bf16[16,64,256]{2,1,0:T(8,128)(2,1)}, u32[]{:S(2)}, u32[]{:S(2)}) collective-permute-start(bf16[16,64,256]{2,1,0:T(8,128)(2,1)} %collective-permute-done.2.r1k), channel_id=1, source_target_pairs={{0,4},{4,8},{8,12},{1,5},{5,9},{9,13},{2,6},{6,10},{10,14},{3,7},{... | collective-permute-start | bytes 1572872 | tf_op jit(solution)/shard_map/ppermute | solution.py:443
  34.2 23.3 %collective-permute-start.5 = (bf16[16,64,256]{2,1,0:T(8,128)(2,1)}, bf16[16,64,256]{2,1,0:T(8,128)(2,1)}, u32[]{:S(2)}, u32[]{:S(2)}) collective-permute-start(bf16[16,64,256]{2,1,0:T(8,128)(2,1)} %collective-permute-done.3.r1o), channel_id=1, source_target_pairs={{0,4},{4,8},{8,12},{1,5},{5,9},{9,13},{2,6},{6,10},{10,14},{3,7},{... | collective-permute-start | bytes 1572872 | tf_op jit(solution)/shard_map/ppermute | solution.py:443
  40.5 40.7 %collective-permute-start.15 = (bf16[16,128,256]{2,1,0:T(8,128)(2,1)}, bf16[16,128,256]{2,1,0:T(8,128)(2,1)}, u32[]{:S(2)}, u32[]{:S(2)}) collective-permute-start(bf16[16,128,256]{2,1,0:T(8,128)(2,1)} %pad_maximum_fusion), channel_id=1, source_target_pairs={{4,0},{8,4},{12,8},{5,1},{9,5},{13,9},{6,2},{10,6},{14,10},{7,3},{... | collective-permute-start | bytes 3145736 | tf_op jit(solution)/shard_map/ppermute | solution.py:443
  57.5 30.8 %copy-start.24 = (s32[4]{0:T(128)S(1)}, s32[4]{0:T(128)}, u32[]{:S(2)}) copy-start(s32[4]{0:T(128)} %add_convert_fusion) | copy-start | bytes 52
  68.1 7.0 %collective-permute-start.7 = (f32[3,4,256]{2,1,0:T(4,128)}, f32[3,4,256]{2,1,0:T(4,128)S(1)}, u32[]{:S(2)}, u32[]{:S(2)}) collective-permute-start(f32[3,4,256]{2,1,0:T(4,128)} %get-tuple-element.14), channel_id=1, source_target_pairs={{0,1},{1,2},{2,3},{4,5},{5,6},{6,7},{8,9},{9,10},{10,11},{12,13},{... | collective-permute-start | bytes 36872 | tf_op jit(solution)/shard_map/ppermute | solution.py:452
  73.2 5.2 %collective-permute-start.8 = (f32[3,4,256]{2,1,0:T(4,128)}, f32[3,4,256]{2,1,0:T(4,128)S(1)}, u32[]{:S(2)}, u32[]{:S(2)}) collective-permute-start(f32[3,4,256]{2,1,0:T(4,128)} %get-tuple-element.15), channel_id=1, source_target_pairs={{1,0},{2,1},{3,2},{5,4},{6,5},{7,6},{9,8},{10,9},{11,10},{13,12},{... | collective-permute-start | bytes 36872 | tf_op jit(solution)/shard_map/ppermute | solution.py:452
  75.1 21.0 %copy-start.18 = (f32[3,4,256]{2,1,0:T(4,128)}, f32[3,4,256]{2,1,0:T(4,128)S(1)}, u32[]{:S(2)}) copy-start(f32[3,4,256]{2,1,0:T(4,128)S(1)} %collective-permute-done.7.above) | copy-start | bytes 36868
  78.4 5.3 %copy-start.19 = (f32[3,4,256]{2,1,0:T(4,128)}, f32[3,4,256]{2,1,0:T(4,128)S(1)}, u32[]{:S(2)}) copy-start(f32[3,4,256]{2,1,0:T(4,128)S(1)} %collective-permute-done.8.below) | copy-start | bytes 36868
  79.1 24.4 %collective-permute-start.9 = (f32[3,24,4]{2,1,0:T(8,128)}, f32[3,24,4]{2,1,0:T(8,128)}, u32[]{:S(2)}, u32[]{:S(2)}) collective-permute-start(f32[3,24,4]{2,1,0:T(8,128)} %pad_maximum_fusion.1), channel_id=1, source_target_pairs={{4,0},{8,4},{12,8},{5,1},{9,5},{13,9},{6,2},{10,6},{14,10},{7,3},{... | collective-permute-start | bytes 3464 | tf_op jit(solution)/shard_map/ppermute | solution.py:443
  81.2 52.7 %collective-permute-start.16 = (bf16[16,128,256]{2,1,0:T(8,128)(2,1)}, bf16[16,128,256]{2,1,0:T(8,128)(2,1)}, u32[]{:S(2)}, u32[]{:S(2)}) collective-permute-start(bf16[16,128,256]{2,1,0:T(8,128)(2,1)} %collective-permute-done.15.l1), channel_id=1, source_target_pairs={{4,0},{8,4},{12,8},{5,1},{9,5},{13,9},{6,2},{10,6},{14,10},{7,3},{... | collective-permute-start | bytes 3145736 | tf_op jit(solution)/shard_map/ppermute | solution.py:443
  83.8 19.8 %collective-permute-start.10 = (f32[3,24,4]{2,1,0:T(8,128)}, f32[3,24,4]{2,1,0:T(8,128)}, u32[]{:S(2)}, u32[]{:S(2)}) collective-permute-start(f32[3,24,4]{2,1,0:T(8,128)} %pad_maximum_fusion.2), channel_id=1, source_target_pairs={{0,4},{4,8},{8,12},{1,5},{5,9},{9,13},{2,6},{6,10},{10,14},{3,7},{... | collective-permute-start | bytes 3464 | tf_op jit(solution)/shard_map/ppermute | solution.py:443
  113.2 17.7 %collective-permute-start.13 = (f32[16,8,256]{2,1,0:T(8,128)}, f32[16,8,256]{2,1,0:T(8,128)S(1)}, u32[]{:S(2)}, u32[]{:S(2)}) collective-permute-start(f32[16,8,256]{2,1,0:T(8,128)} %get-tuple-element.18.coef.coef0), channel_id=1, source_target_pairs={{4,0},{8,4},{12,8},{5,1},{9,5},{13,9},{6,2},{10,6},{14,10},{7,3},{... | collective-permute-start | bytes 393224 | tf_op jit(solution)/shard_map/ppermute | solution.py:443
  115.1 17.0 %collective-permute-start.14 = (f32[16,8,256]{2,1,0:T(8,128)}, f32[16,8,256]{2,1,0:T(8,128)S(1)}, u32[]{:S(2)}, u32[]{:S(2)}) collective-permute-start(f32[16,8,256]{2,1,0:T(8,128)} %get-tuple-element.18.coef.coef0), channel_id=1, source_target_pairs={{8,0},{12,4},{9,1},{13,5},{10,2},{14,6},{11,3},{15,7},{24,16},{28,... | collective-permute-start | bytes 393224 | tf_op jit(solution)/shard_map/ppermute | solution.py:443
  130.8 23.5 %collective-permute-start.12 = (bf16[16,64,256]{2,1,0:T(8,128)(2,1)}, bf16[16,64,256]{2,1,0:T(8,128)(2,1)S(1)}, u32[]{:S(2)}, u32[]{:S(2)}) collective-permute-start(bf16[16,64,256]{2,1,0:T(8,128)(2,1)} %get-tuple-element.20), channel_id=1, source_target_pairs={{0,1},{1,0},{2,3},{3,2},{4,5},{5,4},{6,7},{7,6},{8,9},{9,8},{10,11... | collective-permute-start | bytes 1572872 | tf_op jit(solution)/shard_map/ppermute | solution.py:435
  133.9 18.0 %copy-start.10 = (f32[16,256]{1,0:T(8,128)S(1)}, f32[16,256]{1,0:T(8,128)}, u32[]{:S(2)}) copy-start(f32[16,256]{1,0:T(8,128)} %get-tuple-element.17) | copy-start | bytes 49156
  133.9 20.4 %copy-start.3 = (bf16[16,64,256]{2,1,0:T(8,128)(2,1)S(1)}, bf16[16,64,256]{2,1,0:T(8,128)(2,1)}, u32[]{:S(2)}) copy-start(bf16[16,64,256]{2,1,0:T(8,128)(2,1)} %get-tuple-element.19) | copy-start | bytes 1572868
  151.4 4.1 %collective-permute-start.17 = (bf16[16,64,256]{2,1,0:T(8,128)(2,1)}, bf16[16,64,256]{2,1,0:T(8,128)(2,1)S(1)}, u32[]{:S(2)}, u32[]{:S(2)}) collective-permute-start(bf16[16,64,256]{2,1,0:T(8,128)(2,1)} %get-tuple-element.22), channel_id=1, source_target_pairs={{0,1},{1,0},{2,3},{3,2},{4,5},{5,4},{6,7},{7,6},{8,9},{9,8},{10,11... | collective-permute-start | bytes 1572872 | tf_op jit(solution)/shard_map/ppermute | solution.py:435
  151.9 1.8 %collective-permute-start.11 = (f32[16,128]{1,0:T(8,128)S(1)}, f32[16,128]{1,0:T(8,128)S(1)}, u32[]{:S(2)}, u32[]{:S(2)}) collective-permute-start(f32[16,128]{1,0:T(8,128)S(1)} %get-tuple-element.40), channel_id=1, source_target_pairs={{0,1},{1,0},{2,3},{3,2},{4,5},{5,4},{6,7},{7,6},{8,9},{9,8},{10,11... | collective-permute-start | bytes 24584 | tf_op jit(solution)/shard_map/ppermute | solution.py:435
  (13 other events, 46.1 us)
where the time goes:
time: 158 us; the launch traced here: 157 us
  Pallas kernels  50.6 us (32%)
  starting transfers between devices  33.4 us (21%)
  waiting for transfers between devices  28.1 us (18%)
  local copies, waits for them, and re-layouts  23.1 us (15%)
  other arithmetic  18.2 us (12%)
  between operations  3.14 us (2%)
    ppermute x9, waiting for transfers between devices, over_cols(): return lax.ppermute(a, 'col', pairs)  23.2 us
    ppermute x9, starting transfers between devices, over_cols(): return lax.ppermute(a, 'col', pairs)  22.2 us
    pallas_call x1, Pallas kernels, right_grads(): pl.pallas_call(functools.partial(right_body, chans), name='right_grads',...  17.4 us
    pallas_call x1, Pallas kernels, left_grads(): pl.pallas_call(functools.partial(left_body, chans), name='left_grads', gr...  14.4 us
    add x6, local copies, waits for them, and re-layouts, expand(): sum((jnp.asarray(table[tap])[None, :, None, :, None] * weights[tap][:, No...  10.7 us
    pallas_call x1, Pallas kernels, band_stats(): pl.pallas_call(functools.partial(stats_body, chans), name='band_stats', g...  10.6 us
    pallas_call x1, Pallas kernels, refine(): pl.pallas_call(functools.partial(refine_body, chans, hid), name='refine',...  8.16 us
    ppermute x2, starting transfers between devices, over_rows(): return lax.ppermute(a, ('row', 'ch'), pairs)  6.17 us
  transfers between devices with their start and end apart: 18, of which 5 were waited for; matrix products, arithmetic and copies ran while one was open for 24% of the time, Pallas kernels for 32%

commit v1 on v0

--- a/solution.py
+++ b/solution.py
@@ -39,8 +39,17 @@
     return pl.multiple_of(LANES * block + DISP + 1 - off - rem, ALIGN)
 
 
-def stats_body(chans, off_ref, lk, lo, r0k, r0o, r1k, r1o, r2k, r2o, grad_ref, keep_ref,
-               field, top, bottom, stats, cost, level, mask, lines):
+def softmax_part(scores, lev, rate):
+    top_score = jnp.max(scores, axis=0, keepdims=True)
+    weight = jnp.exp2((scores - top_score) * rate)
+    total = jnp.sum(weight, axis=0, keepdims=True)
+    mean = jnp.sum(weight * lev, axis=0, keepdims=True) / total
+    apart = lev - mean
+    spread = jnp.sum(weight * apart * apart, axis=0, keepdims=True) / total
+    return spread, top_score, mean, total
+
+
+def early_body(chans, off_ref, lk, lo, r0k, r0o, r1k, r1o, lines, cost, level, mask):
     step = pl.program_id(0)
     rate = math.log2(math.e) / math.sqrt(chans)
     off = off_ref[0]
@@ -51,26 +60,47 @@
         lev, msk = band_tables(off)
         level[...] = lev
         mask[...] = msk
-        cost[3 * width:, :] = jnp.zeros((cost.shape[0] - 3 * width, width), F32)
+        cost[:width, :] = jnp.full((width, width), NEG, F32)
+        cost[3 * width:, :] = jnp.full((cost.shape[0] - 3 * width, width), NEG, F32)
 
     @pl.loop(0, GROUP)
     def _(row):
         left = jnp.concatenate([lk[row], lo[row]], axis=0)
-        for slot, (own, other) in enumerate(((r2k, r2o), (r1k, r1o), (r0k, r0o))):
+        for slot, (own, other) in enumerate(((r1k, r1o), (r0k, r0o))):
             right = jnp.concatenate([own[row], other[row]], axis=0)
-            cost[slot * width:(slot + 1) * width, :] = dot(right, left, ((0,), (0,)))
+            cost[(slot + 1) * width:(slot + 2) * width, :] = dot(right, left, ((0,), (0,)))
         line = step * GROUP + row
         for block in range(width // LANES):
             cols = slice(block * LANES, (block + 1) * LANES)
             scores = cost[pl.ds(band_start(off, block), BAND), cols] + mask[...]
-            top_score = jnp.max(scores, axis=0, keepdims=True)
-            weight = jnp.exp2((scores - top_score) * rate)
-            lev = level[...]
-            total = jnp.sum(weight, axis=0, keepdims=True)
-            mean = jnp.sum(weight * lev, axis=0, keepdims=True) / total
-            apart = lev - mean
-            spread = jnp.sum(weight * apart * apart, axis=0, keepdims=True) / total
-            for at, value in enumerate((spread, top_score, mean, 1.0 / total)):
+            for at, value in enumerate(softmax_part(scores, level[...], rate)):
+                lines[line, at:at + 1, cols] = value
+
+
+def late_body(chans, off_ref, lk, lo, rk, ro, early, grad_ref, keep_ref,
+              field, top, bottom, stats, level, mask, lines, planes):
+    step = pl.program_id(0)
+    rate = math.log2(math.e) / math.sqrt(chans)
+    off = off_ref[0]
+    width = lk.shape[2]
+
+    @pl.when(step == 0)
+    def _():
+        across = lax.broadcasted_iota(jnp.int32, (width, width), 1)
+        down = lax.broadcasted_iota(jnp.int32, (width, width), 0)
+        delta = across - down + 2 * width - off
+        level[...] = delta.astype(F32) / DISP
+        mask[...] = jnp.where((delta >= 0) & (delta < DISP), 0.0, NEG).astype(F32)
+
+    for row in range(GROUP):
+        left = jnp.concatenate([lk[row], lo[row]], axis=0)
+        right = jnp.concatenate([rk[row], ro[row]], axis=0)
+        cost = dot(right, left, ((0,), (0,)))
+        line = step * GROUP + row
+        for block in range(width // LANES):
+            cols = slice(block * LANES, (block + 1) * LANES)
+            part = (slice(block * LANES, width), cols)
+            for at, value in enumerate(softmax_part(cost[part] + mask[part], level[part], rate)):
                 lines[line, at:at + 1, cols] = value
 
     rows = field.shape[1]
@@ -79,12 +109,22 @@
     def _():
         for line in range(rows):
             for at in range(4):
-                stats[at + 1, line:line + 1, :] = lines[line, at:at + 1, :]
+                planes[at, line:line + 1, :] = lines[line, at:at + 1, :]
+                planes[at + 4, line:line + 1, :] = early[line, at:at + 1, :]
+        top_score = jnp.maximum(planes[1], planes[5])
+        mass_a = planes[3] * jnp.exp2((planes[1] - top_score) * rate)
+        mass_b = planes[7] * jnp.exp2((planes[5] - top_score) * rate)
+        share = 1.0 / (mass_a + mass_b)
+        mass_a, mass_b = mass_a * share, mass_b * share
+        gap = planes[6] - planes[2]
+        mean = mass_a * planes[2] + mass_b * planes[6]
+        spread = mass_a * planes[0] + mass_b * planes[4] + gap * gap * mass_a * mass_b
         keep = keep_ref[...]
-        coarse = stats[3] + off.astype(F32) / DISP
-        stats[0] = coarse
+        coarse = mean + off.astype(F32) / DISP
+        for at, plane in enumerate((coarse, spread, top_score, mean, share)):
+            stats[at] = plane
         field[0] = coarse * keep
-        field[1] = stats[1] * keep
+        field[1] = spread * keep
         field[2] = grad_ref[...] * keep
         top[...] = field[:, :HALO, :]
         bottom[...] = field[:, rows - HALO:, :]
@@ -105,61 +145,88 @@
     return pl.CostEstimate(flops=flops, bytes_accessed=moved, transcendentals=0)
 
 
-def band_stats(off, left, rights, grad_out, keep):
+def early_stats(off, left, rights):
     rows, half, width = left[0].shape
     chans = 2 * half
     feats = list(left) + [part for pair in rights for part in pair]
-    small = (rows, width)
-    outs = ((3,) + small, (3, HALO, width), (3, HALO, width), (5,) + small)
     return pl.pallas_call(
-        functools.partial(stats_body, chans),
-        name="band_stats",
+        functools.partial(early_body, chans),
+        name="early_stats",
         grid=(rows // GROUP,),
-        in_specs=[SMEM] + [group_spec(a) for a in feats] + [full_spec(small)] * 2,
-        out_specs=[full_spec(s) for s in outs],
-        out_shape=[jax.ShapeDtypeStruct(s, F32) for s in outs],
+        in_specs=[SMEM] + [group_spec(a) for a in feats],
+        out_specs=full_spec((rows, 8, width)),
+        out_shape=jax.ShapeDtypeStruct((rows, 8, width), F32),
         scratch_shapes=[
             pltpu.VMEM((3 * width + ALIGN, width), F32),
             pltpu.VMEM((BAND, LANES), F32),
             pltpu.VMEM((BAND, LANES), F32),
+        ],
+        cost_estimate=cost_of(2 * rows * 3 * width * width * chans, rows * 3 * width * chans * 2),
+    )(off, *feats)
+
+
+def late_stats(off, left, right, early, grad_out, keep):
+    rows, half, width = left[0].shape
+    chans = 2 * half
+    feats = list(left) + list(right)
+    small = (rows, width)
+    outs = ((3,) + small, (3, HALO, width), (3, HALO, width), (5,) + small)
+    return pl.pallas_call(
+        functools.partial(late_body, chans),
+        name="late_stats",
+        grid=(rows // GROUP,),
+        in_specs=[SMEM] + [group_spec(a) for a in feats] + [full_spec(early.shape)]
+        + [full_spec(small)] * 2,
+        out_specs=[full_spec(s) for s in outs],
+        out_shape=[jax.ShapeDtypeStruct(s, F32) for s in outs],
+        scratch_shapes=[
+            pltpu.VMEM((width, width), F32),
+            pltpu.VMEM((width, width), F32),
             pltpu.VMEM((rows, 8, width), F32),
+            pltpu.VMEM((8,) + small, F32),
         ],
-        cost_estimate=cost_of(2 * rows * 3 * width * width * chans, rows * 4 * width * chans * 2),
-    )(off, *feats, grad_out, keep)
+        cost_estimate=cost_of(rows * 3 * width * width * chans, rows * 2 * width * chans * 2),
+    )(off, *feats, early, grad_out, keep)
 
 
 def left_body(chans, off_ref, lk, lo, r0k, r0o, r1k, r1o, r2k, r2o, coef, out_own, out_other,
-              cost, slopes, level, mask):
+              level, mask, tiles, cost, slopes):
     step = pl.program_id(0)
     rate = math.log2(math.e) / math.sqrt(chans)
     off = off_ref[0]
     width = lk.shape[2]
+    parts = width // LANES
+    depth = DISP + 2 * LANES
+    span = depth + width - LANES
+    skip = jnp.where(off < 3 * width - span, 3 * width - span, 0)
 
     @pl.when(step == 0)
     def _():
-        lev, msk = band_tables(off)
-        level[...] = lev
-        mask[...] = msk
-        cost[3 * width:, :] = jnp.zeros((cost.shape[0] - 3 * width, width), F32)
+        across = lax.broadcasted_iota(jnp.int32, (depth, LANES), 1)
+        down = lax.broadcasted_iota(jnp.int32, (depth, LANES), 0)
+        delta = across - down + 2 * width - off - skip
+        level[...] = delta.astype(F32) / DISP
+        mask[...] = jnp.where((delta >= 0) & (delta < DISP), 0.0, NEG).astype(F32)
         slopes[...] = jnp.zeros(slopes.shape, BF16)
 
-    @pl.loop(0, GROUP)
-    def _(row):
+    for row in range(GROUP):
+        for slot, (own, other) in enumerate(((r2k, r2o), (r1k, r1o), (r0k, r0o))):
+            at = slice(slot * width, (slot + 1) * width)
+            tiles[row, :chans // 2, at] = own[row]
+            tiles[row, chans // 2:, at] = other[row]
+    rights = [tiles[row, :, pl.ds(pl.multiple_of(skip, LANES), span)] for row in range(GROUP)]
+    for row, right in enumerate(rights):
         left = jnp.concatenate([lk[row], lo[row]], axis=0)
-        rights = [jnp.concatenate([own[row], other[row]], axis=0)
-                  for own, other in ((r2k, r2o), (r1k, r1o), (r0k, r0o))]
-        for slot, right in enumerate(rights):
-            cost[slot * width:(slot + 1) * width, :] = dot(right, left, ((0,), (0,)))
+        cost[row] = dot(right, left, ((0,), (0,)))
         at = step * GROUP + row
-        for block in range(width // LANES):
+        for block in range(parts):
             cols = slice(block * LANES, (block + 1) * LANES)
-            where = pl.ds(band_start(off, block), BAND)
+            where = slice(block * LANES, block * LANES + depth)
             top_score, mean, one, two, three = (coef[at, f:f + 1, cols] for f in range(5))
-            weight = jnp.exp2((cost[where, cols] + mask[...] - top_score) * rate)
+            weight = jnp.exp2((cost[row, where, cols] + mask[...] - top_score) * rate)
             apart = level[...] - mean
-            slopes[where, cols] = (weight * (apart * (one + two * apart) - three)).astype(BF16)
-        total = sum(dot(right, slopes[slot * width:(slot + 1) * width, :])
-                    for slot, right in enumerate(rights))
+            slopes[row, where, cols] = (weight * (apart * (one + two * apart) - three)).astype(BF16)
+        total = dot(right, slopes[row])
         out_own[row] = total[:chans // 2].astype(BF16)
         out_other[row] = total[chans // 2:].astype(BF16)
 
@@ -168,6 +235,8 @@
     rows, half, width = left[0].shape
     chans = 2 * half
     feats = list(left) + [part for pair in rights for part in pair]
+    depth = DISP + 2 * LANES
+    span = depth + width - LANES
     return pl.pallas_call(
         functools.partial(left_body, chans),
         name="left_grads",
@@ -176,85 +245,84 @@
         out_specs=[group_spec(left[0])] * 2,
         out_shape=[jax.ShapeDtypeStruct(left[0].shape, BF16)] * 2,
         scratch_shapes=[
-            pltpu.VMEM((3 * width + ALIGN, width), F32),
-            pltpu.VMEM((3 * width + ALIGN, width), BF16),
-            pltpu.VMEM((BAND, LANES), F32),
-            pltpu.VMEM((BAND, LANES), F32),
+            pltpu.VMEM((depth, LANES), F32),
+            pltpu.VMEM((depth, LANES), F32),
+            pltpu.VMEM((GROUP, chans, 3 * width), BF16),
+            pltpu.VMEM((GROUP, span, width), F32),
+            pltpu.VMEM((GROUP, span, width), BF16),
         ],
         cost_estimate=cost_of(4 * rows * 3 * width * width * chans, rows * 5 * width * chans * 2),
     )(off, *feats, coef)
 
 
-def right_body(chans, offs_ref, rk, ro, l0k, l0o, l1, l2, coef0, coef1, coef2,
+def right_body(chans, rk, ro, l0k, l0o, l1k, l1o, l2k, l2o, coef0, coef1, coef2,
                out_own, out_other, cost, slopes, mask):
     step = pl.program_id(0)
     rate = math.log2(math.e) / math.sqrt(chans)
     width = rk.shape[2]
     parts = width // LANES
+    coefs = (coef0, coef1, coef2)
     across = lax.broadcasted_iota(jnp.int32, (LANES, LANES), 1)
     down = lax.broadcasted_iota(jnp.int32, (LANES, LANES), 0)
-    blocks = [(tile, col, row) for tile in range(3) for col in range(parts) for row in range(parts)]
-
-    def base_of(tile, col, row):
-        return tile * width + (col - row) * LANES - offs_ref[tile]
+    blocks = [(tile, col, row) for tile in range(3) for col in range(parts) for row in range(parts)
+              if -LANES < tile * width + (col - row) * LANES and
+              tile * width + (col - row) * LANES - width < DISP + LANES]
 
     def spot(tile, col, row):
         return (slice(row * LANES, (row + 1) * LANES),
                 slice(tile * width + col * LANES, tile * width + (col + 1) * LANES))
+
+    def base_of(at, tile, col, row):
+        cols = slice(col * LANES, (col + 1) * LANES)
+        return (tile * width + (col - row) * LANES) - coefs[tile][at, 5:6, cols]
 
     @pl.when(step == 0)
     def _():
         slopes[...] = jnp.zeros(slopes.shape, BF16)
         for tile, col, row in blocks:
-            delta = across - down + base_of(tile, col, row)
+            delta = across - down + base_of(0, tile, col, row).astype(jnp.int32)
             inside = (delta >= 0) & (delta < DISP)
             mask[spot(tile, col, row)] = jnp.where(inside, 0.0, NEG).astype(F32)
 
-    @pl.loop(0, GROUP)
-    def _(line):
+    for line in range(GROUP):
         right = jnp.concatenate([rk[line], ro[line]], axis=0)
-        lefts = [jnp.concatenate([l0k[line], l0o[line]], axis=0), l1[line], l2[line]]
+        lefts = [jnp.concatenate([own[line], other[line]], axis=0)
+                 for own, other in ((l0k, l0o), (l1k, l1o), (l2k, l2o))]
         for tile, left in enumerate(lefts):
-            cost[:, tile * width:(tile + 1) * width] = dot(right, left, ((0,), (0,)))
+            cost[line, :, tile * width:(tile + 1) * width] = dot(right, left, ((0,), (0,)))
         at = step * GROUP + line
         table = (across - down).astype(F32) / DISP
         for tile, col, row in blocks:
-            base = base_of(tile, col, row)
-
-            @pl.when((base + LANES > 0) & (base - LANES < DISP))
-            def _(tile=tile, col=col, row=row, base=base):
-                here = spot(tile, col, row)
-                cols = slice(col * LANES, (col + 1) * LANES)
-                coef = (coef0, coef1, coef2)[tile]
-                top_score, mean, one, two, three = (coef[at, f:f + 1, cols] for f in range(5))
-                weight = jnp.exp2((cost[here] + mask[here] - top_score) * rate)
-                apart = (table + base.astype(F32) / DISP) - mean
-                slopes[here] = (weight * (apart * (one + two * apart) - three)).astype(BF16)
-
-        total = sum(dot(left, slopes[:, tile * width:(tile + 1) * width], ((1,), (1,)))
+            here = spot(tile, col, row)
+            cols = slice(col * LANES, (col + 1) * LANES)
+            top_score, mean, one, two, three = (coefs[tile][at, f:f + 1, cols] for f in range(5))
+            weight = jnp.exp2((cost[(line,) + here] + mask[here] - top_score) * rate)
+            apart = table - (mean - base_of(at, tile, col, row) / DISP)
+            slopes[(line,) + here] = (weight * (apart * (one + two * apart) - three)).astype(BF16)
+        total = sum(dot(left, slopes[line, :, tile * width:(tile + 1) * width], ((1,), (1,)))
                     for tile, left in enumerate(lefts))
         out_own[line] = total[:chans // 2].astype(BF16)
         out_other[line] = total[chans // 2:].astype(BF16)
 
 
-def right_grads(offs, right, left, left_one, left_two, coefs):
+def right_grads(right, lefts, coefs):
     rows, half, width = right[0].shape
     chans = 2 * half
-    feats = list(right) + list(left) + [left_one, left_two]
+    feats = list(right) + [part for pair in lefts for part in pair]
     return pl.pallas_call(
         functools.partial(right_body, chans),
         name="right_grads",
         grid=(rows // GROUP,),
-        in_specs=[SMEM] + [group_spec(a) for a in feats] + [full_spec(a.shape) for a in coefs],
+        in_specs=[group_spec(a) for a in feats] + [full_spec(a.shape) for a in coefs],
         out_specs=[group_spec(right[0])] * 2,
         out_shape=[jax.ShapeDtypeStruct(right[0].shape, BF16)] * 2,
         scratch_shapes=[
-            pltpu.VMEM((width, 3 * width), F32),
-            pltpu.VMEM((width, 3 * width), BF16),
+            pltpu.VMEM((GROUP, width, 3 * width), F32),
+            pltpu.VMEM((GROUP, width, 3 * width), BF16),
             pltpu.VMEM((width, 3 * width), F32),
         ],
         cost_estimate=cost_of(4 * rows * 3 * width * width * chans, rows * 5 * width * chans * 2),
-    )(offs, *feats, *coefs)
+    )(*feats, *coefs)
 
 
 def split_halves(values):
@@ -453,23 +521,23 @@
 
     left_own, left_give = keep_part(left_feat), give_part(left_feat)
     right_own, right_give = keep_part(right_feat), give_part(right_feat)
-    one_own = over_cols(right_own, 1)
-    one_other = crossed(right_give, 1)
-    left_other, right_other = swap(left_give), swap(right_give)
-    left_all = jnp.concatenate([left_own, left_other], axis=1)
-    left_one = over_cols(left_all, -1)
-    two_own = over_cols(one_own, 1)
-    two_other = over_cols(one_other, 1)
-    left_two = over_cols(left_one, -1)
+    right_one = (over_cols(right_own, 1), crossed(right_give, 1))
+    left_one = (over_cols(left_own, -1), crossed(left_give, -1))
+    left = (left_own, swap(left_give))
+    right = (right_own, swap(right_give))
+    right_two = tuple(over_cols(a, 1) for a in right_one)
+    left_two = tuple(over_cols(a, -1) for a in left_one)
 
     maps = jnp.stack([grad_out, valid.astype(F32)])
     maps = joined(keep_part(maps, 1), swap(give_part(maps, 1)), 2)
     grad_map, keep = maps[0], maps[1]
     weights = refine_weights(w_first, w_middle, w_last, rows)
 
-    rights = ((right_own, right_other), (one_own, one_other), (two_own, two_other))
-    left = (left_own, left_other)
-    field, top, bottom, stats = band_stats(offsets, left, rights, grad_map, keep)
+    early = early_stats(offsets, left, (right, right_one))
+    early, right_two, left_two, weights, grad_map, keep = lax.optimization_barrier(
+        (early, right_two, left_two, weights, grad_map, keep))
+    field, top, bottom, stats = late_stats(offsets, left, right_two, early, grad_map, keep)
+    rights = (right, right_one, right_two)
 
     above, below = over_rows(bottom, 1), over_rows(top, -1)
     first = jnp.concatenate([above[:, :, :HALO], field[:, :, :HALO], below[:, :, :HALO]], axis=1)
@@ -484,9 +552,7 @@
     coef_one, coef_two = over_cols(coef, -1), over_cols(coef, -2)
     grad_left = left_grads(offsets, left, rights, coef)
     grad_left = joined(grad_left[0], swap(grad_left[1]), 0)
-    offs = jnp.stack([offsets[0], coef_one[0, 5, 0].astype(jnp.int32),
-                      coef_two[0, 5, 0].astype(jnp.int32)])
-    grad_right = right_grads(offs, rights[0], left, left_one, left_two, (coef, coef_one, coef_two))
+    grad_right = right_grads(right, (left, left_one, left_two), (coef, coef_one, coef_two))
     grad_right = joined(grad_right[0], swap(grad_right[1]), 0)
     refined = joined(keep_part(refined, 1), swap(give_part(refined, 1)), 0)
     return (refined, grad_left, grad_right)

time: 158 us -> 129 us (0.82)
  waiting for transfers between devices: 28.1 us -> 12.4 us
  Pallas kernels: 50.6 us -> 42.5 us
  starting transfers between devices: 33.4 us -> 39.7 us
  other arithmetic: 18.2 us -> 12 us
  local copies, waits for them, and re-layouts: 23.1 us -> 19.3 us
    ppermute x9 -> x10, waiting for transfers between devices: 23.2 us -> 7.54 us  [over_cols(): return lax.ppermute(a, 'col', pairs)]
    pallas_call x1, Pallas kernels: 17.4 us -> 9.09 us  [right_grads(): pl.pallas_call(functools.partial(right_body, chans), name='right_grads',...]
    pallas_call x1 -> x2, Pallas kernels: 10.6 us -> 15.5 us  [the longest x1 10.2 us: early_stats(): pl.pallas_call(functools.partial(early_body, chans), name='early_stats',...]
    pallas_call x1, Pallas kernels: 14.4 us -> 9.76 us  [left_grads(): pl.pallas_call(functools.partial(left_body, chans), name='left_grads', gr...]
    ppermute x9 -> x10, starting transfers between devices: 22.2 us -> 26.7 us  [over_cols(): return lax.ppermute(a, 'col', pairs)]
    add x6 -> x5, local copies, waits for them, and re-layouts: 10.7 us -> 7.63 us  [expand(): sum((jnp.asarray(table[tap])[None, :, None, :, None] * weights[tap][:, No...]
    concatenate x1 -> x0, other arithmetic: 2.26 us -> none  [shards(): left_all = jnp.concatenate([left_own, left_other], axis=1)]
    optimization_barrier x0 -> x2, local copies, waits for them, and re-layouts: none -> 2.08 us  [shards(): lax.optimization_barrier((early, right_two, left_two, weights, grad_map,...]
  transfers between devices with their start and end apart: 18 -> 20, of which waited for: 5 -> 4; matrix products, arithmetic and copies ran while one was open for 24% -> 19% of each run, Pallas kernels for 32% -> 23%
where the time goes in v1:
time: 129 us; the launch traced here: 128 us
  Pallas kernels  42.5 us (33%)
  starting transfers between devices  39.7 us (31%)
  local copies, waits for them, and re-layouts  19.3 us (15%)
  waiting for transfers between devices  12.4 us (10%)
  other arithmetic  12 us (9%)
  between operations  2.05 us (2%)
    ppermute x10, starting transfers between devices, over_cols(): return lax.ppermute(a, 'col', pairs)  26.7 us
    pallas_call x1, Pallas kernels, early_stats(): pl.pallas_call(functools.partial(early_body, chans), name='early_stats',...  10.2 us
    pallas_call x1, Pallas kernels, left_grads(): pl.pallas_call(functools.partial(left_body, chans), name='left_grads', gr...  9.76 us
    pallas_call x1, Pallas kernels, right_grads(): pl.pallas_call(functools.partial(right_body, chans), name='right_grads',...  9.09 us
    pallas_call x1, Pallas kernels, refine(): pl.pallas_call(functools.partial(refine_body, chans, hid), name='refine',...  8.16 us
    add x5, local copies, waits for them, and re-layouts, expand(): sum((jnp.asarray(table[tap])[None, :, None, :, None] * weights[tap][:, No...  7.63 us
    ppermute x10, waiting for transfers between devices, over_cols(): return lax.ppermute(a, 'col', pairs)  7.54 us
    ppermute x2, starting transfers between devices, over_rows(): return lax.ppermute(a, ('row', 'ch'), pairs)  6.05 us
  transfers between devices with their start and end apart: 20, of which 4 were waited for; matrix products, arithmetic and copies ran while one was open for 19% of the time, Pallas kernels for 23%

profile of v1, /device:TPU:17, one launch (start us, length us, event | category | flops | bytes accessed | tf_op | source)
XLA Modules:
  0.0 127.9 jit_solution(15404847265539888068)
XLA Ops:
  0.7 2.4 %constant_dynamic-slice_fusion.4 = (bf16[16,64,256]{2,1,0:T(8,128)(2,1)}, bf16[16,64,256]{2,1,0:T(8,128)(2,1)}) fusion(bf16[32,64,256]{2,1,0:T(8,128)(2,1)} %param.26, s32[]{:T(128)S(6)} %select_n.46, s32[]{:T(128)S(6)} %select_n.45), kind=kLoop, calls=%fused_computation.40 | loop fusion | bytes 2097160 | tf_op jit(solution)/shard_map/dynamic_slice | solution.py:500
  3.9 2.0 %collective-permute-start.8 = (bf16[16,64,256]{2,1,0:T(8,128)(2,1)}, bf16[16,64,256]{2,1,0:T(8,128)(2,1)}, u32[]{:S(2)}, u32[]{:S(2)}) collective-permute-start(bf16[16,64,256]{2,1,0:T(8,128)(2,1)} %get-tuple-element.51), channel_id=1, source_target_pairs={{4,1},{5,0},{8,5},{9,4},{12,9},{13,8},{6,3},{7,2},{10,7},{11,6},{1... | collective-permute-start | bytes 1572872 | tf_op jit(solution)/shard_map/ppermute | solution.py:516
  7.0 4.0 %collective-permute-start.2 = (bf16[16,64,256]{2,1,0:T(8,128)(2,1)}, bf16[16,64,256]{2,1,0:T(8,128)(2,1)}, u32[]{:S(2)}, u32[]{:S(2)}) collective-permute-start(bf16[16,64,256]{2,1,0:T(8,128)(2,1)} %get-tuple-element.50.r0k.rk), channel_id=1, source_target_pairs={{0,4},{4,8},{8,12},{1,5},{5,9},{9,13},{2,6},{6,10},{10,14},{3,7},{... | collective-permute-start | bytes 1572872 | tf_op jit(solution)/shard_map/ppermute | solution.py:511
  11.0 1.9 %collective-permute-start.3 = (bf16[16,64,256]{2,1,0:T(8,128)(2,1)}, bf16[16,64,256]{2,1,0:T(8,128)(2,1)}, u32[]{:S(2)}, u32[]{:S(2)}) collective-permute-start(bf16[16,64,256]{2,1,0:T(8,128)(2,1)} %get-tuple-element.49), channel_id=1, source_target_pairs={{0,5},{1,4},{4,9},{5,8},{8,13},{9,12},{2,7},{3,6},{6,11},{7,10},{1... | collective-permute-start | bytes 1572872 | tf_op jit(solution)/shard_map/ppermute | solution.py:516
  15.3 1.2 add_bitcast_fusion
  17.1 1.6 %multiply_add_fusion.2 = f32[24,32,3,2,24]{1,0,4,3,2:T(8,128)} fusion(f32[32,3,2]{0,2,1:T(2,128)S(1)} %get-tuple-element.76, f32[24,24]{0,1:T(8,128)S(1)} %copy-done.24, f32[32,3,2]{0,2,1:T(2,128)S(1)} %get-tuple-element.75, f32[24,24]{0,1:T(8,128)S(1)} %copy-done.23, f32[32,3,2]{0,2,1:T(2,128)S(1)} %get-tuple-element.74, f32[24,24]{0,1:T(8,128)S(1)} %copy-done.22), kind=kLoop, calls=%fused_computation.2 | loop fusion | flops 552960 | bytes 451584 | tf_op jit(solution)/shard_map/add | solution.py:437
  19.1 3.3 %collective-permute-start.6 = (bf16[16,64,256]{2,1,0:T(8,128)(2,1)}, bf16[16,64,256]{2,1,0:T(8,128)(2,1)}, u32[]{:S(2)}, u32[]{:S(2)}) collective-permute-start(bf16[16,64,256]{2,1,0:T(8,128)(2,1)} %get-tuple-element.52.lk.l0k), channel_id=1, source_target_pairs={{4,0},{8,4},{12,8},{5,1},{9,5},{13,9},{6,2},{10,6},{14,10},{7,3},{... | collective-permute-start | bytes 1572872 | tf_op jit(solution)/shard_map/ppermute | solution.py:511
  22.4 1.7 %multiply_add_fusion.1 = f32[3,5,32,7,32]{4,3,2,1,0:T(8,128)} fusion(f32[3,32,32]{2,1,0:T(8,128)S(1)} %get-tuple-element.58, f32[5,7]{1,0:T(8,128)S(1)} %copy-done.33, f32[3,32,32]{2,1,0:T(8,128)S(1)} %get-tuple-element.57, f32[5,7]{1,0:T(8,128)S(1)} %copy-done.32, f32[3,32,32]{2,1,0:T(8,128)S(1)} %get-tuple-element.56, f32[5,7]{1,0:T(8,128)S(1)} %copy-done.31), kind=kLoop, calls=%fused_computation.1 | loop fusion | flops 537600 | bytes 467364 | tf_op jit(solution)/shard_map/add | solution.py:437
  26.6 2.1 %reshape.160 = f32[640,72]{0,1:T(8,128)} reshape(f32[20,32,3,1,24]{1,0,4,2,3:T(8,128)} %add_bitcast_fusion) | data formatting | bytes 368640 | tf_op jit(solution)/shard_map/reshape | solution.py:452
  28.6 1.9 %add.120.w_three = f32[48,576]{1,0:T(8,128)} reshape(f32[3,16,18,32]{3,2,1,0:T(8,128)} %multiply_add_fusion.4) | data formatting | bytes 221184 | tf_op jit(solution)/shard_map/add | solution.py:437
  30.5 1.5 %add.125.w_two_back = f32[576,256]{1,0:T(8,128)} reshape(f32[3,6,32,8,32]{4,3,2,1,0:T(8,128)S(1)} %multiply_add_fusion) | data formatting | bytes 1179648 | tf_op jit(solution)/shard_map/add | solution.py:437
  32.0 2.8 %add.117.w_two = f32[480,224]{1,0:T(8,128)} reshape(f32[3,5,32,7,32]{4,3,2,1,0:T(8,128)} %multiply_add_fusion.1) | data formatting | bytes 860160 | tf_op jit(solution)/shard_map/add | solution.py:437
  36.3 3.5 %collective-permute-start.4 = (bf16[16,64,256]{2,1,0:T(8,128)(2,1)}, bf16[16,64,256]{2,1,0:T(8,128)(2,1)S(1)}, u32[]{:S(2)}, u32[]{:S(2)}) collective-permute-start(bf16[16,64,256]{2,1,0:T(8,128)(2,1)} %collective-permute-done.2.r1k), channel_id=1, source_target_pairs={{0,4},{4,8},{8,12},{1,5},{5,9},{9,13},{2,6},{6,10},{10,14},{3,7},{... | collective-permute-start | bytes 1572872 | tf_op jit(solution)/shard_map/ppermute | solution.py:511
  39.9 1.9 %collective-permute-start.7 = (bf16[16,64,256]{2,1,0:T(8,128)(2,1)}, bf16[16,64,256]{2,1,0:T(8,128)(2,1)S(1)}, u32[]{:S(2)}, u32[]{:S(2)}) collective-permute-start(bf16[16,64,256]{2,1,0:T(8,128)(2,1)} %collective-permute-done.6.l1k), channel_id=1, source_target_pairs={{4,0},{8,4},{12,8},{5,1},{9,5},{13,9},{6,2},{10,6},{14,10},{7,3},{... | collective-permute-start | bytes 1572872 | tf_op jit(solution)/shard_map/ppermute | solution.py:511
  41.8 3.4 %collective-permute-start.5 = (bf16[16,64,256]{2,1,0:T(8,128)(2,1)}, bf16[16,64,256]{2,1,0:T(8,128)(2,1)S(1)}, u32[]{:S(2)}, u32[]{:S(2)}) collective-permute-start(bf16[16,64,256]{2,1,0:T(8,128)(2,1)} %collective-permute-done.3.r1o), channel_id=1, source_target_pairs={{0,4},{4,8},{8,12},{1,5},{5,9},{9,13},{2,6},{6,10},{10,14},{3,7},{... | collective-permute-start | bytes 1572872 | tf_op jit(solution)/shard_map/ppermute | solution.py:511
  45.2 1.9 %collective-permute-start.9 = (bf16[16,64,256]{2,1,0:T(8,128)(2,1)}, bf16[16,64,256]{2,1,0:T(8,128)(2,1)S(1)}, u32[]{:S(2)}, u32[]{:S(2)}) collective-permute-start(bf16[16,64,256]{2,1,0:T(8,128)(2,1)} %collective-permute-done.8.l1o), channel_id=1, source_target_pairs={{4,0},{8,4},{12,8},{5,1},{9,5},{13,9},{6,2},{10,6},{14,10},{7,3},{... | collective-permute-start | bytes 1572872 | tf_op jit(solution)/shard_map/ppermute | solution.py:511
  48.6 10.2 %early_stats.1.early = f32[16,8,256]{2,1,0:T(8,128)} custom-call(s32[1]{0:T(128)S(6)} %copy.75.off_ref, bf16[16,64,256]{2,1,0:T(8,128)(2,1)} %get-tuple-element.52.lk.l0k, bf16[16,64,256]{2,1,0:T(8,128)(2,1)} %collective-permute-done.lo.l0o, bf16[16,64,256]{2,1,0:T(8,128)(2,1)} %get-tuple-element.50.r0k.rk, ...), custom_call_target="tpu_custom_call" | custom-call | flops 805306368 | bytes 3145728 | tf_op jit(solution)/shard_map/early_stats/pallas_call | solution.py:152
  58.9 4.2 %collective-permute-done.5.ro.r2o = bf16[16,64,256]{2,1,0:T(8,128)(2,1)S(1)} collective-permute-done((bf16[16,64,256]{2,1,0:T(8,128)(2,1)}, bf16[16,64,256]{2,1,0:T(8,128)(2,1)S(1)}, u32[]{:S(2)}, u32[]{:S(2)}) %collective-permute-start.5) | collective-permute-done | bytes 524320 | tf_op jit(solution)/shard_map/ppermute | solution.py:511
  63.1 3.3 %collective-permute-done.9.l2o = bf16[16,64,256]{2,1,0:T(8,128)(2,1)S(1)} collective-permute-done((bf16[16,64,256]{2,1,0:T(8,128)(2,1)}, bf16[16,64,256]{2,1,0:T(8,128)(2,1)S(1)}, u32[]{:S(2)}, u32[]{:S(2)}) %collective-permute-start.9) | collective-permute-done | bytes 524320 | tf_op jit(solution)/shard_map/ppermute | solution.py:511
  66.4 5.3 %late_stats.1 = (f32[3,16,256]{2,1,0:T(8,128)}, f32[3,4,256]{2,1,0:T(4,128)}, f32[3,4,256]{2,1,0:T(4,128)}, f32[5,16,256]{2,1,0:T(8,128)}) custom-call(s32[1]{0:T(128)S(6)} %copy.75.off_ref, bf16[16,64,256]{2,1,0:T(8,128)(2,1)} %get-tuple-element.52.lk.l0k, bf16[16,64,256]{2,1,0:T(8,128)(2,1)} %collective-permute-done.lo.l0o, ...), custom_call_target="tpu_custom_call" | custom-call | flops 402653184 | bytes 2097152 | tf_op jit(solution)/shard_map/late_stats/pallas_call | solution.py:174
  71.7 4.1 %collective-permute-start.11 = (f32[3,4,256]{2,1,0:T(4,128)}, f32[3,4,256]{2,1,0:T(4,128)S(1)}, u32[]{:S(2)}, u32[]{:S(2)}) collective-permute-start(f32[3,4,256]{2,1,0:T(4,128)} %get-tuple-element.32), channel_id=1, source_target_pairs={{0,1},{1,2},{2,3},{4,5},{5,6},{6,7},{8,9},{9,10},{10,11},{12,13},{... | collective-permute-start | bytes 36872 | tf_op jit(solution)/shard_map/ppermute | solution.py:520
  76.7 1.9 %collective-permute-start.12 = (f32[3,4,256]{2,1,0:T(4,128)}, f32[3,4,256]{2,1,0:T(4,128)S(1)}, u32[]{:S(2)}, u32[]{:S(2)}) collective-permute-start(f32[3,4,256]{2,1,0:T(4,128)} %get-tuple-element.33), channel_id=1, source_target_pairs={{1,0},{2,1},{3,2},{5,4},{6,5},{7,6},{9,8},{10,9},{11,10},{13,12},{... | collective-permute-start | bytes 36872 | tf_op jit(solution)/shard_map/ppermute | solution.py:520
  78.7 3.2 %collective-permute-done.12.below = f32[3,4,256]{2,1,0:T(4,128)S(1)} collective-permute-done((f32[3,4,256]{2,1,0:T(4,128)}, f32[3,4,256]{2,1,0:T(4,128)S(1)}, u32[]{:S(2)}, u32[]{:S(2)}) %collective-permute-start.12) | collective-permute-done | bytes 12320 | tf_op jit(solution)/shard_map/ppermute | solution.py:520
  82.0 1.9 %collective-permute-start.13 = (f32[3,24,4]{2,1,0:T(8,128)S(1)}, f32[3,24,4]{2,1,0:T(8,128)S(1)}, u32[]{:S(2)}, u32[]{:S(2)}) collective-permute-start(f32[3,24,4]{2,1,0:T(8,128)S(1)} %pad_maximum_fusion), channel_id=1, source_target_pairs={{4,0},{8,4},{12,8},{5,1},{9,5},{13,9},{6,2},{10,6},{14,10},{7,3},{... | collective-permute-start | bytes 3464 | tf_op jit(solution)/shard_map/ppermute | solution.py:511
  83.9 3.5 %collective-permute-start.14 = (f32[3,24,4]{2,1,0:T(8,128)S(1)}, f32[3,24,4]{2,1,0:T(8,128)S(1)}, u32[]{:S(2)}, u32[]{:S(2)}) collective-permute-start(f32[3,24,4]{2,1,0:T(8,128)S(1)} %pad_maximum_fusion.1), channel_id=1, source_target_pairs={{0,4},{4,8},{8,12},{1,5},{5,9},{9,13},{2,6},{6,10},{10,14},{3,7},{... | collective-permute-start | bytes 3464 | tf_op jit(solution)/shard_map/ppermute | solution.py:511
  88.2 1.1 copy.59.w_one
  91.0 8.2 %refine.1 = (f32[16,256]{1,0:T(8,128)}, f32[16,8,256]{2,1,0:T(8,128)}) custom-call(s32[5]{0:T(128)} %pad_add_fusion.flags, f32[3,16,256]{2,1,0:T(8,128)} %get-tuple-element.31.field, f32[3,4,256]{2,1,0:T(4,128)} %copy-done.28, f32[3,4,256]{2,1,0:T(4,128)} %copy-done.29, f32[3,24,128]{2,1,0:T(8,128)} %pad_maximum_fusion.2.side, ...), custom_call_target="tpu_custom_call" | custom-call | flops 4000000000 | bytes 8000000 | tf_op jit(solution)/shard_map/refine/pallas_call | solution.py:473
  99.1 1.9 %collective-permute-start.17 = (f32[16,8,256]{2,1,0:T(8,128)}, f32[16,8,256]{2,1,0:T(8,128)S(1)}, u32[]{:S(2)}, u32[]{:S(2)}) collective-permute-start(f32[16,8,256]{2,1,0:T(8,128)} %get-tuple-element.42.coef.coef0), channel_id=1, source_target_pairs={{4,0},{8,4},{12,8},{5,1},{9,5},{13,9},{6,2},{10,6},{14,10},{7,3},{... | collective-permute-start | bytes 393224 | tf_op jit(solution)/shard_map/ppermute | solution.py:511
  101.1 1.3 %collective-permute-start.18 = (f32[16,8,256]{2,1,0:T(8,128)}, f32[16,8,256]{2,1,0:T(8,128)S(1)}, u32[]{:S(2)}, u32[]{:S(2)}) collective-permute-start(f32[16,8,256]{2,1,0:T(8,128)} %get-tuple-element.42.coef.coef0), channel_id=1, source_target_pairs={{8,0},{12,4},{9,1},{13,5},{10,2},{14,6},{11,3},{15,7},{24,16},{28,... | collective-permute-start | bytes 393224 | tf_op jit(solution)/shard_map/ppermute | solution.py:511
  102.4 9.8 %left_grads.1 = (bf16[16,64,256]{2,1,0:T(8,128)(2,1)}, bf16[16,64,256]{2,1,0:T(8,128)(2,1)}) custom-call(s32[1]{0:T(128)S(6)} %copy.75.off_ref, bf16[16,64,256]{2,1,0:T(8,128)(2,1)} %get-tuple-element.52.lk.l0k, bf16[16,64,256]{2,1,0:T(8,128)(2,1)} %collective-permute-done.lo.l0o, bf16[16,64,256]{2,1,0:T(8,128)(2,1)} %get-tuple-element.50.r0k.rk, ...), custom_call_target="tpu_custom_call" | custom-call | flops 1610612736 | bytes 5242880 | tf_op jit(solution)/shard_map/left_grads/pallas_call | solution.py:240
  113.6 9.1 %right_grads.1 = (bf16[16,64,256]{2,1,0:T(8,128)(2,1)}, bf16[16,64,256]{2,1,0:T(8,128)(2,1)}) custom-call(bf16[16,64,256]{2,1,0:T(8,128)(2,1)} %get-tuple-element.50.r0k.rk, bf16[16,64,256]{2,1,0:T(8,128)(2,1)} %collective-permute-done.1.r0o.ro, bf16[16,64,256]{2,1,0:T(8,128)(2,1)} %get-tuple-element.52.lk.l0k, ...), custom_call_target="tpu_custom_call" | custom-call | flops 1610612736 | bytes 5242880 | tf_op jit(solution)/shard_map/right_grads/pallas_call | solution.py:312
  123.4 1.6 %collective-permute-done.15 = f32[16,128]{1,0:T(8,128)S(1)} collective-permute-done((f32[16,128]{1,0:T(8,128)S(1)}, f32[16,128]{1,0:T(8,128)S(1)}, u32[]{:S(2)}, u32[]{:S(2)}) %collective-permute-start.15) | collective-permute-done | bytes 8224 | tf_op jit(solution)/shard_map/ppermute | solution.py:503
  (146 shorter events, 18.0 us)
Async XLA Ops:
  0.7 12.3 %copy-start.15 = (f32[32,128]{1,0:T(8,128)S(1)}, f32[32,128]{1,0:T(8,128)}, u32[]{:S(2)}) copy-start(f32[32,128]{1,0:T(8,128)} %param.33) | copy-start | bytes 49156
  0.7 13.6 %copy-start.9 = (f32[3,3,32,2]{2,3,1,0:T(2,128)S(1)}, f32[3,3,32,2]{2,3,1,0:T(2,128)}, u32[]{:S(2)}) copy-start(f32[3,3,32,2]{2,3,1,0:T(2,128)} %param.30) | copy-start | bytes 6916
  0.7 13.6 %copy-start.30 = (f32[3,3,1,32]{3,2,1,0:T(1,128)S(1)}, f32[3,3,1,32]{3,2,1,0:T(1,128)}, u32[]{:S(2)}) copy-start(f32[3,3,1,32]{3,2,1,0:T(1,128)} %param.32) | copy-start | bytes 3460
  0.7 14.3 %copy-start.3 = (f32[3,3,32,32]{3,2,1,0:T(8,128)S(1)}, f32[3,3,32,32]{3,2,1,0:T(8,128)}, u32[]{:S(2)}) copy-start(f32[3,3,32,32]{3,2,1,0:T(8,128)} %param.31) | copy-start | bytes 110596
  3.1 13.4 %copy-start.34 = (f32[6,8]{1,0:T(8,128)S(1)}, f32[6,8]{1,0:T(8,128)}, u32[]{:S(2)}) copy-start(f32[6,8]{1,0:T(8,128)} %constant.71.clone) | copy-start | bytes 580
  3.1 13.4 %copy-start.35 = (f32[6,8]{1,0:T(8,128)S(1)}, f32[6,8]{1,0:T(8,128)}, u32[]{:S(2)}) copy-start(f32[6,8]{1,0:T(8,128)} %constant.72.clone) | copy-start | bytes 580
  3.1 13.4 %copy-start.36 = (f32[6,8]{1,0:T(8,128)S(1)}, f32[6,8]{1,0:T(8,128)}, u32[]{:S(2)}) copy-start(f32[6,8]{1,0:T(8,128)} %constant.73.clone) | copy-start | bytes 580
  3.1 33.1 %collective-permute-start = (bf16[16,64,256]{2,1,0:T(8,128)(2,1)}, bf16[16,64,256]{2,1,0:T(8,128)(2,1)}, u32[]{:S(2)}, u32[]{:S(2)}) collective-permute-start(bf16[16,64,256]{2,1,0:T(8,128)(2,1)} %get-tuple-element.51), channel_id=1, source_target_pairs={{0,1},{1,0},{2,3},{3,2},{4,5},{5,4},{6,7},{7,6},{8,9},{9,8},{10,11... | collective-permute-start | bytes 1572872 | tf_op jit(solution)/shard_map/ppermute | solution.py:503
  3.9 41.3 %collective-permute-start.8 = (bf16[16,64,256]{2,1,0:T(8,128)(2,1)}, bf16[16,64,256]{2,1,0:T(8,128)(2,1)}, u32[]{:S(2)}, u32[]{:S(2)}) collective-permute-start(bf16[16,64,256]{2,1,0:T(8,128)(2,1)} %get-tuple-element.51), channel_id=1, source_target_pairs={{4,1},{5,0},{8,5},{9,4},{12,9},{13,8},{6,3},{7,2},{10,7},{11,6},{1... | collective-permute-start | bytes 1572872 | tf_op jit(solution)/shard_map/ppermute | solution.py:516
  7.0 17.1 %collective-permute-start.2 = (bf16[16,64,256]{2,1,0:T(8,128)(2,1)}, bf16[16,64,256]{2,1,0:T(8,128)(2,1)}, u32[]{:S(2)}, u32[]{:S(2)}) collective-permute-start(bf16[16,64,256]{2,1,0:T(8,128)(2,1)} %get-tuple-element.50.r0k.rk), channel_id=1, source_target_pairs={{0,4},{4,8},{8,12},{1,5},{5,9},{9,13},{2,6},{6,10},{10,14},{3,7},{... | collective-permute-start | bytes 1572872 | tf_op jit(solution)/shard_map/ppermute | solution.py:511
  11.0 30.8 %collective-permute-start.3 = (bf16[16,64,256]{2,1,0:T(8,128)(2,1)}, bf16[16,64,256]{2,1,0:T(8,128)(2,1)}, u32[]{:S(2)}, u32[]{:S(2)}) collective-permute-start(bf16[16,64,256]{2,1,0:T(8,128)(2,1)} %get-tuple-element.49), channel_id=1, source_target_pairs={{0,5},{1,4},{4,9},{5,8},{8,13},{9,12},{2,7},{3,6},{6,11},{7,10},{1... | collective-permute-start | bytes 1572872 | tf_op jit(solution)/shard_map/ppermute | solution.py:516
  13.5 5.5 %collective-permute-start.10 = (f32[2,16,128]{2,1,0:T(8,128)}, f32[2,16,128]{2,1,0:T(8,128)}, u32[]{:S(2)}, u32[]{:S(2)}) collective-permute-start(f32[2,16,128]{2,1,0:T(8,128)} %get-tuple-element.64), channel_id=1, source_target_pairs={{0,1},{1,0},{2,3},{3,2},{4,5},{5,4},{6,7},{7,6},{8,9},{9,8},{10,11... | collective-permute-start | bytes 49160 | tf_op jit(solution)/shard_map/ppermute | solution.py:503
  19.1 20.8 %collective-permute-start.6 = (bf16[16,64,256]{2,1,0:T(8,128)(2,1)}, bf16[16,64,256]{2,1,0:T(8,128)(2,1)}, u32[]{:S(2)}, u32[]{:S(2)}) collective-permute-start(bf16[16,64,256]{2,1,0:T(8,128)(2,1)} %get-tuple-element.52.lk.l0k), channel_id=1, source_target_pairs={{4,0},{8,4},{12,8},{5,1},{9,5},{13,9},{6,2},{10,6},{14,10},{7,3},{... | collective-permute-start | bytes 1572872 | tf_op jit(solution)/shard_map/ppermute | solution.py:511
  24.1 24.5 %collective-permute-start.1 = (bf16[16,64,256]{2,1,0:T(8,128)(2,1)}, bf16[16,64,256]{2,1,0:T(8,128)(2,1)}, u32[]{:S(2)}, u32[]{:S(2)}) collective-permute-start(bf16[16,64,256]{2,1,0:T(8,128)(2,1)} %get-tuple-element.49), channel_id=1, source_target_pairs={{0,1},{1,0},{2,3},{3,2},{4,5},{5,4},{6,7},{7,6},{8,9},{9,8},{10,11... | collective-permute-start | bytes 1572872 | tf_op jit(solution)/shard_map/ppermute | solution.py:503
  36.3 22.5 %collective-permute-start.4 = (bf16[16,64,256]{2,1,0:T(8,128)(2,1)}, bf16[16,64,256]{2,1,0:T(8,128)(2,1)S(1)}, u32[]{:S(2)}, u32[]{:S(2)}) collective-permute-start(bf16[16,64,256]{2,1,0:T(8,128)(2,1)} %collective-permute-done.2.r1k), channel_id=1, source_target_pairs={{0,4},{4,8},{8,12},{1,5},{5,9},{9,13},{2,6},{6,10},{10,14},{3,7},{... | collective-permute-start | bytes 1572872 | tf_op jit(solution)/shard_map/ppermute | solution.py:511
  39.9 19.0 %collective-permute-start.7 = (bf16[16,64,256]{2,1,0:T(8,128)(2,1)}, bf16[16,64,256]{2,1,0:T(8,128)(2,1)S(1)}, u32[]{:S(2)}, u32[]{:S(2)}) collective-permute-start(bf16[16,64,256]{2,1,0:T(8,128)(2,1)} %collective-permute-done.6.l1k), channel_id=1, source_target_pairs={{4,0},{8,4},{12,8},{5,1},{9,5},{13,9},{6,2},{10,6},{14,10},{7,3},{... | collective-permute-start | bytes 1572872 | tf_op jit(solution)/shard_map/ppermute | solution.py:511
  41.8 21.3 %collective-permute-start.5 = (bf16[16,64,256]{2,1,0:T(8,128)(2,1)}, bf16[16,64,256]{2,1,0:T(8,128)(2,1)S(1)}, u32[]{:S(2)}, u32[]{:S(2)}) collective-permute-start(bf16[16,64,256]{2,1,0:T(8,128)(2,1)} %collective-permute-done.3.r1o), channel_id=1, source_target_pairs={{0,4},{4,8},{8,12},{1,5},{5,9},{9,13},{2,6},{6,10},{10,14},{3,7},{... | collective-permute-start | bytes 1572872 | tf_op jit(solution)/shard_map/ppermute | solution.py:511
  45.2 21.2 %collective-permute-start.9 = (bf16[16,64,256]{2,1,0:T(8,128)(2,1)}, bf16[16,64,256]{2,1,0:T(8,128)(2,1)S(1)}, u32[]{:S(2)}, u32[]{:S(2)}) collective-permute-start(bf16[16,64,256]{2,1,0:T(8,128)(2,1)} %collective-permute-done.8.l1o), channel_id=1, source_target_pairs={{4,0},{8,4},{12,8},{5,1},{9,5},{13,9},{6,2},{10,6},{14,10},{7,3},{... | collective-permute-start | bytes 1572872 | tf_op jit(solution)/shard_map/ppermute | solution.py:511
  58.8 30.5 %copy-start.2 = (f32[640,72]{0,1:T(8,128)S(1)}, f32[640,72]{0,1:T(8,128)}, u32[]{:S(2)}) copy-start(f32[640,72]{0,1:T(8,128)} %reshape.160) | copy-start | bytes 552964
  58.9 40.3 %copy-start.37 = (bf16[16,64,256]{2,1,0:T(8,128)(2,1)}, bf16[16,64,256]{2,1,0:T(8,128)(2,1)S(1)}, u32[]{:S(2)}) copy-start(bf16[16,64,256]{2,1,0:T(8,128)(2,1)S(1)} %collective-permute-done.7.l2k) | copy-start | bytes 1572868
  66.4 23.9 %copy-start.38 = (bf16[16,64,256]{2,1,0:T(8,128)(2,1)}, bf16[16,64,256]{2,1,0:T(8,128)(2,1)S(1)}, u32[]{:S(2)}) copy-start(bf16[16,64,256]{2,1,0:T(8,128)(2,1)S(1)} %collective-permute-done.9.l2o) | copy-start | bytes 1572868
  71.7 6.9 %collective-permute-start.11 = (f32[3,4,256]{2,1,0:T(4,128)}, f32[3,4,256]{2,1,0:T(4,128)S(1)}, u32[]{:S(2)}, u32[]{:S(2)}) collective-permute-start(f32[3,4,256]{2,1,0:T(4,128)} %get-tuple-element.32), channel_id=1, source_target_pairs={{0,1},{1,2},{2,3},{4,5},{5,6},{6,7},{8,9},{9,10},{10,11},{12,13},{... | collective-permute-start | bytes 36872 | tf_op jit(solution)/shard_map/ppermute | solution.py:520
  76.7 5.2 %collective-permute-start.12 = (f32[3,4,256]{2,1,0:T(4,128)}, f32[3,4,256]{2,1,0:T(4,128)S(1)}, u32[]{:S(2)}, u32[]{:S(2)}) collective-permute-start(f32[3,4,256]{2,1,0:T(4,128)} %get-tuple-element.33), channel_id=1, source_target_pairs={{1,0},{2,1},{3,2},{5,4},{6,5},{7,6},{9,8},{10,9},{11,10},{13,12},{... | collective-permute-start | bytes 36872 | tf_op jit(solution)/shard_map/ppermute | solution.py:520
  78.6 12.4 %copy-start.28 = (f32[3,4,256]{2,1,0:T(4,128)}, f32[3,4,256]{2,1,0:T(4,128)S(1)}, u32[]{:S(2)}) copy-start(f32[3,4,256]{2,1,0:T(4,128)S(1)} %collective-permute-done.11.above) | copy-start | bytes 36868
  82.0 8.3 %collective-permute-start.13 = (f32[3,24,4]{2,1,0:T(8,128)S(1)}, f32[3,24,4]{2,1,0:T(8,128)S(1)}, u32[]{:S(2)}, u32[]{:S(2)}) collective-permute-start(f32[3,24,4]{2,1,0:T(8,128)S(1)} %pad_maximum_fusion), channel_id=1, source_target_pairs={{4,0},{8,4},{12,8},{5,1},{9,5},{13,9},{6,2},{10,6},{14,10},{7,3},{... | collective-permute-start | bytes 3464 | tf_op jit(solution)/shard_map/ppermute | solution.py:511
  83.9 6.3 %collective-permute-start.14 = (f32[3,24,4]{2,1,0:T(8,128)S(1)}, f32[3,24,4]{2,1,0:T(8,128)S(1)}, u32[]{:S(2)}, u32[]{:S(2)}) collective-permute-start(f32[3,24,4]{2,1,0:T(8,128)S(1)} %pad_maximum_fusion.1), channel_id=1, source_target_pairs={{0,4},{4,8},{8,12},{1,5},{5,9},{9,13},{2,6},{6,10},{10,14},{3,7},{... | collective-permute-start | bytes 3464 | tf_op jit(solution)/shard_map/ppermute | solution.py:511
  99.1 13.1 %collective-permute-start.17 = (f32[16,8,256]{2,1,0:T(8,128)}, f32[16,8,256]{2,1,0:T(8,128)S(1)}, u32[]{:S(2)}, u32[]{:S(2)}) collective-permute-start(f32[16,8,256]{2,1,0:T(8,128)} %get-tuple-element.42.coef.coef0), channel_id=1, source_target_pairs={{4,0},{8,4},{12,8},{5,1},{9,5},{13,9},{6,2},{10,6},{14,10},{7,3},{... | collective-permute-start | bytes 393224 | tf_op jit(solution)/shard_map/ppermute | solution.py:511
  101.1 11.2 %collective-permute-start.18 = (f32[16,8,256]{2,1,0:T(8,128)}, f32[16,8,256]{2,1,0:T(8,128)S(1)}, u32[]{:S(2)}, u32[]{:S(2)}) collective-permute-start(f32[16,8,256]{2,1,0:T(8,128)} %get-tuple-element.42.coef.coef0), channel_id=1, source_target_pairs={{8,0},{12,4},{9,1},{13,5},{10,2},{14,6},{11,3},{15,7},{24,16},{28,... | collective-permute-start | bytes 393224 | tf_op jit(solution)/shard_map/ppermute | solution.py:511
  112.2 13.5 %copy-start.7 = (bf16[16,64,256]{2,1,0:T(8,128)(2,1)S(1)}, bf16[16,64,256]{2,1,0:T(8,128)(2,1)}, u32[]{:S(2)}) copy-start(bf16[16,64,256]{2,1,0:T(8,128)(2,1)} %get-tuple-element.43) | copy-start | bytes 1572868
  112.2 13.4 %collective-permute-start.16 = (bf16[16,64,256]{2,1,0:T(8,128)(2,1)}, bf16[16,64,256]{2,1,0:T(8,128)(2,1)S(1)}, u32[]{:S(2)}, u32[]{:S(2)}) collective-permute-start(bf16[16,64,256]{2,1,0:T(8,128)(2,1)} %get-tuple-element.44), channel_id=1, source_target_pairs={{0,1},{1,0},{2,3},{3,2},{4,5},{5,4},{6,7},{7,6},{8,9},{9,8},{10,11... | collective-permute-start | bytes 1572872 | tf_op jit(solution)/shard_map/ppermute | solution.py:503
  122.7 4.1 %collective-permute-start.19 = (bf16[16,64,256]{2,1,0:T(8,128)(2,1)}, bf16[16,64,256]{2,1,0:T(8,128)(2,1)S(1)}, u32[]{:S(2)}, u32[]{:S(2)}) collective-permute-start(bf16[16,64,256]{2,1,0:T(8,128)(2,1)} %get-tuple-element.48), channel_id=1, source_target_pairs={{0,1},{1,0},{2,3},{3,2},{4,5},{5,4},{6,7},{7,6},{8,9},{9,8},{10,11... | collective-permute-start | bytes 1572872 | tf_op jit(solution)/shard_map/ppermute | solution.py:503
  123.3 1.8 %collective-permute-start.15 = (f32[16,128]{1,0:T(8,128)S(1)}, f32[16,128]{1,0:T(8,128)S(1)}, u32[]{:S(2)}, u32[]{:S(2)}) collective-permute-start(f32[16,128]{1,0:T(8,128)S(1)} %get-tuple-element.66), channel_id=1, source_target_pairs={{0,1},{1,0},{2,3},{3,2},{4,5},{5,4},{6,7},{7,6},{8,9},{9,8},{10,11... | collective-permute-start | bytes 24584 | tf_op jit(solution)/shard_map/ppermute | solution.py:503
  (29 other events, 142.1 us)
